TPU v7x, 128 devices: a whole 4x4x4 slice. The times are simulated.
128 devices in a mesh: gx: 4 (over y), gy: 4 (over x), gz: 8 (over z, core).
Axes of the slice: x: 4, y: 4, z: 4, core: 2. Of those that a mesh axis runs over, the one named last changes fastest.
Arguments:
- point_feats: bfloat16 [32, 1048576], P(None, ('gx', 'gy', 'gz')), may hold values from -40 to 40
- voxel_ids: int32 [1048576], P(('gx', 'gy', 'gz')), may hold values from 0 to 4095
- send_counts: int32 [128, 128], P(('gx', 'gy', 'gz')), may hold values from 0 to 64, as said below
- active: int32 [16, 16, 2048], P('gx', 'gy', 'gz'), may hold values from 0 to 1
- w_sub: bfloat16 [64, 864], replicated, may hold values from -0.21875 to 0.21875
- w_down: bfloat16 [64, 512], replicated, may hold values from -0.25 to 0.25
- bn_gain: float32 [64], replicated, may hold values from 0.4 to 1.6
- bn_shift: float32 [64], replicated, may hold values from -2.5 to 2.5
- cotangent: bfloat16 [64, 8, 8, 1024], P(None, 'gx', 'gy', 'gz'), may hold values from -6 to 6
Outputs:
- coarse_out: bfloat16 [64, 8, 8, 1024], P(None, 'gx', 'gy', 'gz')
- grad_points: bfloat16 [32, 1048576], P(None, ('gx', 'gy', 'gz'))
- grad_sub: float32 [64, 864], replicated
- grad_down: float32 [64, 512], replicated
- grad_gain: float32 [64], replicated
- grad_shift: float32 [64], replicated
Inputs may be any that keep to these rules, and one draw needn't show every extreme that they name: The slots for destination d are the 64 slots from d * 64 on; the first send_counts[src, d] of them hold points. Some destination device gets 64 points from every source device.
All inputs are finite; a program needn't handle non-finite values.
Results may differ from a plain program's by a relative error of at most 0.009.
Values may be sent and summed in bfloat16 or wider, within the bound.
A program may use at most 192 MiB of HBM per device.

v0:
```python
import jax
import jax.numpy as jnp
from jax import lax
from jax.sharding import PartitionSpec as P

EPS = 1e-05


def padded_2(cells, sides, width):
    for axis, dim in sides:
        count = lax.axis_size(axis)
        ends = count - 1
        head = lax.slice_in_dim(cells, 0, width, axis=dim)
        tail = lax.slice_in_dim(cells, cells.shape[dim] - width, cells.shape[dim], axis=dim)
        cells = jnp.concatenate(
            [
                lax.ppermute(tail, axis, [(i, (i + 1) % count) for i in range(ends)]),
                cells,
                lax.ppermute(head, axis, [((i + 1) % count, i) for i in range(ends)]),
            ],
            axis=dim,
        )
    return cells


def columns(padded, start_x, start_y, size_x, size_y, size_z, starts_z):
    pieces = [
        padded[
            :, start_x : start_x + size_x, start_y : start_y + size_y, start_z : start_z + size_z
        ]
        for start_z in starts_z
    ]
    joined = jnp.concatenate(pieces, axis=0)
    return joined.reshape(joined.shape[0], size_x * size_y * size_z)


def on_device(
    point_feats, voxel_ids, send_counts, active, w_sub, w_down, bn_gain, bn_shift, cotangent
):
    in_chan, slot_total = point_feats.shape
    devices = send_counts.shape[1]
    slot_cap = slot_total // devices
    size_x, size_y, size_z = active.shape
    volume = size_x * size_y * size_z
    out_chan = w_sub.shape[0]
    slot_rank = jnp.arange(slot_cap, dtype=jnp.int32)
    usable = (slot_rank[None, :] < send_counts[0][:, None]).reshape(1, slot_total)
    outgoing = jnp.where(usable, point_feats, jnp.zeros_like(point_feats))
    voxel_tags = jnp.where(usable, voxel_ids.reshape(1, slot_total), -1)
    arriving, arrived_tags = (
        lax.all_to_all(outgoing, ("gx", "gy", "gz"), split_axis=1, concat_axis=1, tiled=True),
        lax.all_to_all(voxel_tags, ("gx", "gy", "gz"), split_axis=1, concat_axis=1, tiled=True),
    )
    landed = arrived_tags[0] >= 0
    target = jnp.where(landed, arrived_tags[0], 0)
    summed = jax.ops.segment_sum(arriving.T.astype(jnp.float32), target, num_segments=volume)
    activity = active.reshape(1, volume).astype(jnp.float32)
    grid_in = (summed.T * activity).astype(jnp.bfloat16).reshape(in_chan, size_x, size_y, size_z)
    padded = padded_2(grid_in, (("gx", 1), ("gy", 2), ("gz", 3)), 1)
    conv_sum = jnp.zeros((out_chan, volume), jnp.float32)
    for start_x in range(3):
        for start_y in range(3):
            first = (start_x * 3 + start_y) * 3 * in_chan
            stacked = columns(padded, start_x, start_y, size_x, size_y, size_z, (0, 1, 2))
            conv_sum = conv_sum + jnp.dot(
                w_sub[:, first : first + 3 * in_chan], stacked, preferred_element_type=jnp.float32
            )
    hidden = conv_sum * activity
    totals, active_count = lax.psum(
        (jnp.sum(hidden, axis=1), jnp.sum(activity)), ("gx", "gy", "gz")
    )
    average = totals / active_count
    centred = (hidden - average[:, None]) * activity
    spread = lax.psum(jnp.sum(centred * centred, axis=1), ("gx", "gy", "gz"))
    variance = spread / active_count
    inverse = lax.rsqrt(variance + EPS)
    normed = (hidden - average[:, None]) * inverse[:, None]
    pre_act = bn_gain[:, None] * normed + bn_shift[:, None]
    gelu_val, gelu_back = jax.vjp(jax.nn.gelu, pre_act)
    fine_out = (gelu_val * activity).astype(jnp.bfloat16)
    half_x, half_y, half_z = (size_x // 2, size_y // 2, size_z // 2)
    coarse_active = (
        active.reshape(half_x, 2, half_y, 2, half_z, 2).max(axis=(1, 3, 5)).reshape(1, -1)
    )
    fine_stack = (
        fine_out.reshape(out_chan, half_x, 2, half_y, 2, half_z, 2)
        .transpose(2, 4, 6, 0, 1, 3, 5)
        .reshape(8 * out_chan, -1)
    )
    coarse_sum = jnp.dot(
        w_down, fine_stack, preferred_element_type=jnp.float32
    ) * coarse_active.astype(jnp.float32)
    coarse_out = coarse_sum.astype(jnp.bfloat16).reshape(out_chan, half_x, half_y, half_z)
    grad_c = cotangent.reshape(out_chan, -1) * coarse_active.astype(jnp.bfloat16)
    local_down = lax.dot_general(
        grad_c, fine_stack, (((1,), (1,)), ((), ())), preferred_element_type=jnp.float32
    )
    grad_stack = jnp.dot(w_down.T, grad_c, preferred_element_type=jnp.float32)
    grad_fine = (
        grad_stack.reshape(2, 2, 2, out_chan, half_x, half_y, half_z)
        .transpose(3, 4, 0, 5, 1, 6, 2)
        .reshape(out_chan, volume)
    )
    grad_pre = gelu_back(grad_fine * activity)[0]
    raw_shift, raw_gain = lax.psum(
        (jnp.sum(grad_pre, axis=1), jnp.sum(grad_pre * normed, axis=1)), ("gx", "gy", "gz")
    )
    grad_hidden = (
        activity
        * (bn_gain * inverse)[:, None]
        * (grad_pre - (raw_shift[:, None] + normed * raw_gain[:, None]) / active_count)
    )
    grad_hidden = grad_hidden.astype(jnp.bfloat16)
    w_blocks = w_sub.reshape(out_chan, 27, in_chan)
    sub_parts = []
    tap_groups = []
    for start_x in range(3):
        for start_y in range(3):
            stacked = columns(padded, start_x, start_y, size_x, size_y, size_z, (0, 1, 2))
            sub_parts.append(
                lax.dot_general(
                    grad_hidden,
                    stacked,
                    (((1,), (1,)), ((), ())),
                    preferred_element_type=jnp.float32,
                )
            )
            group = (start_x * 3 + start_y) * 3
            tap_groups.append(
                w_blocks[:, group : group + 3, :].transpose(2, 1, 0).reshape(in_chan, 3 * out_chan)
            )
    local_sub = jnp.concatenate(sub_parts, axis=1)
    grad_cube = grad_hidden.reshape(out_chan, size_x, size_y, size_z)
    grad_padded = padded_2(grad_cube, (("gx", 1), ("gy", 2), ("gz", 3)), 1)
    back_sum = jnp.zeros((in_chan, volume), jnp.float32)
    for start_x in range(3):
        for start_y in range(3):
            shifted = columns(
                grad_padded, 2 - start_x, 2 - start_y, size_x, size_y, size_z, (2, 1, 0)
            )
            back_sum = back_sum + jnp.dot(
                tap_groups[start_x * 3 + start_y], shifted, preferred_element_type=jnp.float32
            )
    grad_grid = (back_sum * activity).astype(jnp.bfloat16)
    grad_slots = jnp.where(landed[None, :], grad_grid[:, target], jnp.zeros((), jnp.bfloat16))
    returned = lax.all_to_all(
        grad_slots, ("gx", "gy", "gz"), split_axis=1, concat_axis=1, tiled=True
    )
    raw_sub, raw_down = lax.psum((local_sub, local_down), ("gx", "gy", "gz"))
    grad_scale = lax.rsqrt(active_count)
    return (
        coarse_out,
        returned,
        raw_sub * grad_scale,
        raw_down * grad_scale,
        raw_gain * grad_scale,
        raw_shift * grad_scale,
    )


def solution(mesh):
    in_specs = (
        P(None, ("gx", "gy", "gz")),
        P(("gx", "gy", "gz")),
        P(("gx", "gy", "gz"), None),
        P("gx", "gy", "gz"),
        P(),
        P(),
        P(),
        P(),
        P(None, "gx", "gy", "gz"),
    )
    out_specs = (P(None, "gx", "gy", "gz"), P(None, ("gx", "gy", "gz")), P(), P(), P(), P())
    return jax.shard_map(
        on_device, mesh=mesh, in_specs=in_specs, out_specs=out_specs, check_vma=False
    )
```

profile of v0, /device:TPU:1, one launch (start us, length us, event | category | flops | bytes accessed | tf_op | source)
XLA Modules:
  0.0 583.2 jit_solution(4788719559351473196)
XLA Ops:
  9.6 11.5 %all-to-all-start = ((s32[1,128,64]{2,0,1:T(1,128)}), s32[1,128,64]{2,0,1:T(1,128)S(1)}, u32[]{:S(2)}, u32[]{:S(2)}) async-start(s32[1,128,64]{2,0,1:T(1,128)} %bitcast.1), calls=%async_computation | async-start | bytes 131072 | tf_op jit(solution)/shard_map/all_to_all | solution.py:52
  40.9 9.8 %all-to-all-start.1 = ((bf16[128,2,1024]{2,1,0:T(2,128)(2,1)}), bf16[128,2,1024]{2,1,0:T(2,128)(2,1)S(1)}, u32[]{:S(2)}, u32[]{:S(2)}) async-start(bf16[128,2,1024]{2,1,0:T(2,128)(2,1)} %reshape.317), calls=%async_computation.1 | async-start | bytes 1048576 | tf_op jit(solution)/shard_map/all_to_all | solution.py:51
  53.3 11.0 %all-to-all-done.1 = bf16[128,2,1024]{2,1,0:T(2,128)(2,1)S(1)} async-done(((bf16[128,2,1024]{2,1,0:T(2,128)(2,1)}), bf16[128,2,1024]{2,1,0:T(2,128)(2,1)S(1)}, u32[]{:S(2)}, u32[]{:S(2)}) %all-to-all-start.1) | async-done | bytes 524320 | tf_op jit(solution)/shard_map/all_to_all | solution.py:51
  67.0 2.7 copy.176
  69.7 50.6 %scatter_custom_fusion = f32[4096,32]{1,0:T(8,128)S(1)} fusion(s32[8192]{0:T(1024)S(1)} %bitcast.141, f32[8192,32]{1,0:T(8,128)} %copy.176, f32[]{:T(128)} %constant.13.clone.1), kind=kCustom, calls=%fused_computation.75 | custom fusion | flops 262144 | bytes 524800 | tf_op jit(solution)/shard_map/scatter-add | solution.py:56
  124.7 3.5 collective-permute-done.1
  133.7 3.8 collective-permute-done.3
  138.4 5.4 collective-permute-start.4
  148.4 4.4 collective-permute-done.5
  155.5 4.1 fusion.73
  185.6 2.9 reshape.256
  196.1 62.8 %all-reduce.1 = (f32[64]{0:T(128)S(1)}, f32[]{:T(128)}) all-reduce(f32[64]{0:T(128)S(1)} %get-tuple-element.103, f32[]{:T(128)} %convert_reduce_fusion), channel_id=1, replica_groups=mesh['gx'=4,'gy'=4,'gz'=8] {'gx','gy','gz'}, use_global_device_ids=true, to_apply=%region_2.3 | all-reduce | flops 65 | bytes 520 | tf_op jit(solution)/shard_map/psum | solution.py:69
  260.5 63.2 %psum.51 = f32[64]{0:T(128)S(1)} all-reduce(f32[64]{0:T(128)S(1)} %multiply_reduce_fusion), channel_id=1, replica_groups=mesh['gx'=4,'gy'=4,'gz'=8] {'gx','gy','gz'}, use_global_device_ids=true, to_apply=%region_6.7 | all-reduce | flops 64 | bytes 512 | tf_op jit(solution)/shard_map/psum | solution.py:74
  324.3 3.6 fusion.67
  328.0 63.5 %all-reduce = (f32[64]{0:T(128)S(1)}, f32[64]{0:T(128)S(1)}) all-reduce(f32[64]{0:T(128)S(1)} %get-tuple-element.7, f32[64]{0:T(128)S(1)} %get-tuple-element.6), channel_id=1, replica_groups=mesh['gx'=4,'gy'=4,'gz'=8] {'gx','gy','gz'}, use_global_device_ids=true, to_apply=%region_11.12 | all-reduce | flops 128 | bytes 1024 | tf_op jit(solution)/shard_map/psum | solution.py:105
  405.7 4.0 collective-permute-start.6
  420.2 3.6 collective-permute-done.9
  426.9 4.4 collective-permute-start.11
  441.3 3.5 fusion.70
  454.9 2.9 reshape.287
  461.4 3.9 reshape.281
  472.4 3.9 reshape.278
  479.9 4.1 reshape.276
  487.5 3.9 reshape.271
  496.3 3.8 reshape.285
  500.2 3.8 copy.196
  504.0 3.8 reshape.274
  507.8 3.8 copy.207
  511.6 3.8 reshape.283
  527.3 24.0 %gather_fusion = bf16[8192,32]{1,0:T(8,128)(2,1)S(1)} fusion(bf16[32,4096]{0,1:T(8,128)(2,1)S(1)} %copy.214, s32[8192]{0:T(1024)S(1)} %copy-done.61), kind=kCustom, calls=%fused_computation | custom fusion | bytes 1081344 | tf_op jit(solution)/shard_map/gather | solution.py:145
  553.8 6.0 %all-to-all-start.2 = ((bf16[128,2,1024]{2,1,0:T(2,128)(2,1)}), bf16[128,2,1024]{2,1,0:T(2,128)(2,1)S(1)}, u32[]{:S(2)}, u32[]{:S(2)}) async-start(bf16[128,2,1024]{2,1,0:T(2,128)(2,1)} %reshape.319), calls=%async_computation.2 | async-start | bytes 1048576 | tf_op jit(solution)/shard_map/all_to_all | solution.py:146
  564.2 9.2 %all-to-all-done.2 = bf16[128,2,1024]{2,1,0:T(2,128)(2,1)S(1)} async-done(((bf16[128,2,1024]{2,1,0:T(2,128)(2,1)}), bf16[128,2,1024]{2,1,0:T(2,128)(2,1)S(1)}, u32[]{:S(2)}, u32[]{:S(2)}) %all-to-all-start.2) | async-done | bytes 524320 | tf_op jit(solution)/shard_map/all_to_all | solution.py:146
  (361 shorter events, 171.5 us)
Async XLA Ops:
  7.2 18.5 %copy-start = (bf16[64,512]{1,0:T(8,128)(2,1)S(1)}, bf16[64,512]{1,0:T(8,128)(2,1)}, u32[]{:S(2)}) copy-start(bf16[64,512]{1,0:T(8,128)(2,1)} %param.14) | copy-start | bytes 196612
  7.2 17.3 %copy-start.44 = (bf16[64,864]{1,0:T(8,128)(2,1)S(1)}, bf16[64,864]{1,0:T(8,128)(2,1)}, u32[]{:S(2)}) copy-start(bf16[64,864]{1,0:T(8,128)(2,1)} %param.13) | copy-start | bytes 331780
  7.2 17.5 %copy-start.50 = (bf16[32,8192]{1,0:T(8,128)(2,1)S(1)}, bf16[32,8192]{1,0:T(8,128)(2,1)}, u32[]{:S(2)}) copy-start(bf16[32,8192]{1,0:T(8,128)(2,1)} %param.9) | copy-start | bytes 1572868
  9.6 31.4 %all-to-all-start = ((s32[1,128,64]{2,0,1:T(1,128)}), s32[1,128,64]{2,0,1:T(1,128)S(1)}, u32[]{:S(2)}, u32[]{:S(2)}) async-start(s32[1,128,64]{2,0,1:T(1,128)} %bitcast.1), calls=%async_computation | async-start | bytes 131072 | tf_op jit(solution)/shard_map/all_to_all | solution.py:52
  40.9 23.3 %all-to-all-start.1 = ((bf16[128,2,1024]{2,1,0:T(2,128)(2,1)}), bf16[128,2,1024]{2,1,0:T(2,128)(2,1)S(1)}, u32[]{:S(2)}, u32[]{:S(2)}) async-start(bf16[128,2,1024]{2,1,0:T(2,128)(2,1)} %reshape.317), calls=%async_computation.1 | async-start | bytes 1048576 | tf_op jit(solution)/shard_map/all_to_all | solution.py:51
  50.7 510.3 %all-reduce.5.cloned.1.call-start = ((), (), s32[]{:S(2)}) async-start(), calls=%async_computation.3 | async-start | bytes 720896 | tf_op jit(solution)/shard_map/psum | solution.py:149
  121.2 3.3 collective-permute-start
  123.2 5.0 collective-permute-start.1
  124.5 9.2 %copy-start.54 = (bf16[32,1,4,256]{3,2,1,0:T(4,128)(2,1)}, bf16[32,1,4,256]{3,2,1,0:T(4,128)(2,1)S(1)}, u32[]{:S(2)}) copy-start(bf16[32,1,4,256]{3,2,1,0:T(4,128)(2,1)S(1)} %collective-permute-done) | copy-start | bytes 196612
  128.2 10.1 %copy-start.56 = (bf16[32,1,4,256]{3,2,1,0:T(4,128)(2,1)}, bf16[32,1,4,256]{3,2,1,0:T(4,128)(2,1)S(1)}, u32[]{:S(2)}) copy-start(bf16[32,1,4,256]{3,2,1,0:T(4,128)(2,1)S(1)} %collective-permute-done.1) | copy-start | bytes 196612
  128.6 5.1 collective-permute-start.2
  131.1 6.4 %collective-permute-start.3 = (bf16[32,6,1,256]{3,2,1,0:T(2,128)(2,1)S(1)}, bf16[32,6,1,256]{3,2,1,0:T(2,128)(2,1)S(1)}, u32[]{:S(2)}, u32[]{:S(2)}) collective-permute-start(bf16[32,6,1,256]{3,2,1,0:T(2,128)(2,1)S(1)} %get-tuple-element.85), channel_id=1, source_target_pairs={{8,0},{16,8},{24,16},{9,1},{17,9},{25,17},{10,2},{18,10},{26,18},{... | collective-permute-start | bytes 294920 | tf_op jit(solution)/shard_map/ppermute | solution.py:19
  138.4 10.1 %collective-permute-start.4 = (bf16[32,6,6,1]{3,2,1,0:T(8,128)(2,1)S(1)}, bf16[32,6,6,1]{3,2,1,0:T(8,128)(2,1)S(1)}, u32[]{:S(2)}, u32[]{:S(2)}) collective-permute-start(bf16[32,6,6,1]{3,2,1,0:T(8,128)(2,1)S(1)} %get-tuple-element.70), channel_id=1, source_target_pairs={{0,1},{1,2},{2,3},{3,4},{4,5},{5,6},{6,7},{8,9},{9,10},{10,11},{11... | collective-permute-start | bytes 6920 | tf_op jit(solution)/shard_map/ppermute | solution.py:17
  143.7 9.1 %collective-permute-start.5 = (bf16[32,6,6,1]{3,2,1,0:T(8,128)(2,1)S(1)}, bf16[32,6,6,1]{3,2,1,0:T(8,128)(2,1)S(1)}, u32[]{:S(2)}, u32[]{:S(2)}) collective-permute-start(bf16[32,6,6,1]{3,2,1,0:T(8,128)(2,1)S(1)} %get-tuple-element.71), channel_id=1, source_target_pairs={{1,0},{2,1},{3,2},{4,3},{5,4},{6,5},{7,6},{9,8},{10,9},{11,10},{12... | collective-permute-start | bytes 6920 | tf_op jit(solution)/shard_map/ppermute | solution.py:19
  165.8 27.2 %copy-start.2 = (bf16[96,4096]{1,0:T(8,128)(2,1)}, bf16[96,4096]{1,0:T(8,128)(2,1)S(1)}, u32[]{:S(2)}) copy-start(bf16[96,4096]{1,0:T(8,128)(2,1)S(1)} %reshape.259) | copy-start | bytes 2359300
  168.4 23.2 %copy-start.4 = (bf16[96,4096]{1,0:T(8,128)(2,1)}, bf16[96,4096]{1,0:T(8,128)(2,1)S(1)}, u32[]{:S(2)}) copy-start(bf16[96,4096]{1,0:T(8,128)(2,1)S(1)} %reshape.258) | copy-start | bytes 2359300
  176.2 4.7 copy-start.55
  195.6 128.0 %copy-start.83 = (f32[64]{0:T(128)S(1)}, f32[64]{0:T(128)}, u32[]{:S(2)}) copy-start(f32[64]{0:T(128)} %param.15) | copy-start | bytes 772
  195.7 128.7 %copy-start.88 = (f32[64]{0:T(128)S(1)}, f32[64]{0:T(128)}, u32[]{:S(2)}) copy-start(f32[64]{0:T(128)} %param.16) | copy-start | bytes 772
  403.1 6.6 %copy-start.34 = (bf16[64,4096]{1,0:T(8,128)(2,1)S(1)}, bf16[64,4096]{1,0:T(8,128)(2,1)}, u32[]{:S(2)}) copy-start(bf16[64,4096]{1,0:T(8,128)(2,1)} %get-tuple-element.57) | copy-start | bytes 1572868
  403.7 6.6 %copy-start.19 = (bf16[64,4,4,256]{3,0,2,1:T(8,128)(2,1)}, bf16[64,4,4,256]{3,0,2,1:T(8,128)(2,1)S(1)}, u32[]{:S(2)}) copy-start(bf16[64,4,4,256]{3,0,2,1:T(8,128)(2,1)S(1)} %copy.185) | copy-start | bytes 1572868
  404.4 9.8 %collective-permute-start.7 = (bf16[64,1,4,256]{3,0,2,1:T(8,128)(2,1)}, bf16[64,1,4,256]{3,0,2,1:T(8,128)(2,1)S(1)}, u32[]{:S(2)}, u32[]{:S(2)}) collective-permute-start(bf16[64,1,4,256]{3,0,2,1:T(8,128)(2,1)} %get-tuple-element.78), channel_id=1, source_target_pairs={{32,0},{64,32},{96,64},{33,1},{65,33},{97,65},{34,2},{66,34},{98,6... | collective-permute-start | bytes 393224 | tf_op jit(solution)/shard_map/ppermute | solution.py:19
  405.7 8.3 %collective-permute-start.6 = (bf16[64,1,4,256]{3,0,2,1:T(8,128)(2,1)}, bf16[64,1,4,256]{3,0,2,1:T(8,128)(2,1)S(1)}, u32[]{:S(2)}, u32[]{:S(2)}) collective-permute-start(bf16[64,1,4,256]{3,0,2,1:T(8,128)(2,1)} %get-tuple-element.79), channel_id=1, source_target_pairs={{0,32},{32,64},{64,96},{1,33},{33,65},{65,97},{2,34},{34,66},{66,9... | collective-permute-start | bytes 393224 | tf_op jit(solution)/shard_map/ppermute | solution.py:17
  413.2 5.1 copy-start.87
  414.9 5.3 collective-permute-start.8
  417.0 6.8 %collective-permute-start.9 = (bf16[64,6,1,256]{3,0,2,1:T(8,128)(2,1)S(1)}, bf16[64,6,1,256]{3,0,2,1:T(8,128)(2,1)S(1)}, u32[]{:S(2)}, u32[]{:S(2)}) collective-permute-start(bf16[64,6,1,256]{3,0,2,1:T(8,128)(2,1)S(1)} %get-tuple-element.67), channel_id=1, source_target_pairs={{8,0},{16,8},{24,16},{9,1},{17,9},{25,17},{10,2},{18,10},{26,18},{... | collective-permute-start | bytes 589832 | tf_op jit(solution)/shard_map/ppermute | solution.py:19
  426.9 10.7 %collective-permute-start.11 = (bf16[64,6,6,1]{0,2,3,1:T(8,128)(2,1)S(1)}, bf16[64,6,6,1]{0,2,3,1:T(8,128)(2,1)S(1)}, u32[]{:S(2)}, u32[]{:S(2)}) collective-permute-start(bf16[64,6,6,1]{0,2,3,1:T(8,128)(2,1)S(1)} %copy.218), channel_id=1, source_target_pairs={{0,1},{1,2},{2,3},{3,4},{4,5},{5,6},{6,7},{8,9},{9,10},{10,11},{11... | collective-permute-start | bytes 13832 | tf_op jit(solution)/shard_map/ppermute | solution.py:17
  431.3 5.2 collective-permute-start.10
  479.9 4.1 copy-start.30
  552.4 7.4 %copy-start.85 = (f32[64]{0:T(128)S(1)}, f32[64]{0:T(128)}, u32[]{:S(2)}) copy-start(f32[64]{0:T(128)} %copy-done.84) | copy-start | bytes 772
  552.4 7.9 %copy-start.53 = (bf16[64,512]{1,0:T(8,128)(2,1)S(1)}, bf16[64,512]{1,0:T(8,128)(2,1)}, u32[]{:S(2)}) copy-start(bf16[64,512]{1,0:T(8,128)(2,1)} %fusion.18) | copy-start | bytes 196612
  553.8 19.6 %all-to-all-start.2 = ((bf16[128,2,1024]{2,1,0:T(2,128)(2,1)}), bf16[128,2,1024]{2,1,0:T(2,128)(2,1)S(1)}, u32[]{:S(2)}, u32[]{:S(2)}) async-start(bf16[128,2,1024]{2,1,0:T(2,128)(2,1)} %reshape.319), calls=%async_computation.2 | async-start | bytes 1048576 | tf_op jit(solution)/shard_map/all_to_all | solution.py:146
  (73 other events, 146.3 us)
Sparse Core Ops, SparseCore 0:
  413.3 141.5 all-reduce.4
where the time goes:
time: 591 us; the launch traced here: 583 us
  blocking collectives  189 us (32%)
  local copies, waits for them, and re-layouts  158 us (27%)
  other arithmetic  99.2 us (17%)
  starting transfers between devices  57.1 us (10%)
  waiting for transfers between devices  39.4 us (7%)
  matrix products  23.5 us (4%)
  between operations  16.3 us (3%)
    psum x1, blocking collectives, on_device(): lax.psum((jnp.sum(grad_pre, axis=1), jnp.sum(grad_pre * normed, axis=1)),...  63.5 us
    psum x1, blocking collectives, on_device(): spread = lax.psum(jnp.sum(centred * centred, axis=1), ('gx', 'gy', 'gz'))  63.2 us
    psum x1, blocking collectives, on_device(): lax.psum((jnp.sum(hidden, axis=1), jnp.sum(activity)), ('gx', 'gy', 'gz'))  62.8 us
    scatter-add x1, other arithmetic, on_device(): jax.ops.segment_sum(arriving.T.astype(jnp.float32), target, num_segments=...  50.6 us
    reshape x16, local copies, waits for them, and re-layouts, columns(): return joined.reshape(joined.shape[0], size_x * size_y * size_z)  43.3 us
    concatenate x12, local copies, waits for them, and re-layouts, columns(): joined = jnp.concatenate(pieces, axis=0)  28.2 us
    gather x2, local copies, waits for them, and re-layouts, on_device(): grad_grid[:, target]  25 us
    concatenate x12, other arithmetic, columns(): joined = jnp.concatenate(pieces, axis=0)  21.5 us
  transfers between devices with their start and end apart: 16, of which 10 were waited for; matrix products, arithmetic and copies ran while one was open for 25% of the time, Pallas kernels for 0%

commit v1 on v0

v1 whole, which is shorter than its diff:
```python
import functools

import jax
import jax.numpy as jnp
from jax import lax
from jax.experimental import pallas as pl
from jax.experimental.pallas import tpu as pltpu
from jax.sharding import PartitionSpec as P

EPS = 1e-05
TANH_SCALE = 0.7978845608028654
TANH_CUBE = 0.044715
F32 = jnp.float32
BF16 = jnp.bfloat16
LOGICAL = pl.DeviceIdType.LOGICAL
VMEM = pl.BlockSpec(memory_space=pltpu.VMEM)
NT = (((1,), (1,)), ((), ()))
CHUNK = 1024
GX, GY, GZ = 4, 4, 8
N_DEV = GX * GY * GZ
N_XY = GX * GY


def place():
    return lax.axis_index("gx"), lax.axis_index("gy"), lax.axis_index("gz")


def flat_id(ix, iy, iz):
    return (ix * GY + iy) * GZ + iz


def iota(shape, dim):
    return lax.broadcasted_iota(jnp.int32, shape, dim)


def drain(ref, sem):
    pltpu.make_async_copy(ref, ref, sem).wait()


def send(src, dst, send_sem, recv_sem, device):
    pltpu.make_async_remote_copy(
        src_ref=src,
        dst_ref=dst,
        send_sem=send_sem,
        recv_sem=recv_sem,
        device_id=device,
        device_id_type=LOGICAL,
    ).start()


def greet_all(me, barrier):
    def body(step, carry):
        pl.semaphore_signal(
            barrier, inc=1, device_id=lax.rem(me + step, N_DEV), device_id_type=LOGICAL
        )
        return carry

    lax.fori_loop(1, N_DEV, body, 0)


def halves(first, second):
    return jnp.concatenate([first[:, :64], second[:, :64]], axis=1), jnp.concatenate(
        [first[:, 64:], second[:, 64:]], axis=1
    )


def route_kernel(
    feats_ref, ids_ref, counts_ref, x_ref, tags_ref,
    out_buf, in_buf, out_ids, in_ids, send_sem, recv_sem,
):
    ix, iy, iz = place()
    me = flat_id(ix, iy, iz)
    barrier = pltpu.get_barrier_semaphore()
    greet_all(me, barrier)
    row, lane = iota((64, 128), 0), iota((64, 128), 1)
    counts = counts_ref[...]
    even = jnp.sum(jnp.where(lane == 2 * row, counts, 0), axis=1, keepdims=True)
    odd = jnp.sum(jnp.where(lane == 2 * row + 1, counts, 0), axis=1, keepdims=True)
    usable = (lane & 63) < jnp.where(lane < 64, even, odd)
    tags = jnp.where(usable, ids_ref[...], -1)
    for m in range(64):
        out_ids[m] = tags[m : m + 1]

    def pack(m, carry):
        block = feats_ref[:, pl.ds(pl.multiple_of(m * 128, 128), 128)]
        first, second = halves(block[:16], block[16:])
        out_buf[2 * m] = first
        out_buf[2 * m + 1] = second
        return carry

    lax.fori_loop(0, 64, pack, 0)
    pl.semaphore_wait(barrier, N_DEV - 1)

    def go(step, carry):
        to = lax.rem(me + step, N_DEV)
        send(out_buf.at[to], in_buf.at[me], send_sem.at[0], recv_sem.at[0], to)
        send(out_ids.at[lax.div(to, 2)], in_ids.at[me], send_sem.at[1], recv_sem.at[1], to)
        return carry

    lax.fori_loop(1, N_DEV, go, 0)
    in_buf[me] = out_buf[me]
    in_ids[me] = out_ids[lax.div(me, 2)]
    most = pl.ds(0, N_DEV - 1)
    drain(in_buf.at[most], recv_sem.at[0])
    drain(in_ids.at[most], recv_sem.at[1])
    low = iota((1, 128), 1) < 64
    first_core = lax.rem(me, 2) == 0

    def unpack(m, carry):
        top, bottom = halves(in_buf[2 * m], in_buf[2 * m + 1])
        at = pl.ds(pl.multiple_of(m * 128, 128), 128)
        x_ref[0:16, at] = top
        x_ref[16:32, at] = bottom
        one, two = in_ids[2 * m], in_ids[2 * m + 1]
        in_first = jnp.where(low, one, pltpu.roll(two, 64, 1))
        in_second = jnp.where(low, pltpu.roll(one, 64, 1), two)
        tags_ref[pl.ds(m, 1), :] = jnp.where(first_core, in_first, in_second)
        return carry

    lax.fori_loop(0, 64, unpack, 0)
    drain(out_buf.at[most], send_sem.at[0])
    drain(in_ids.at[most], send_sem.at[1])


def route(feats, ids, counts):
    return pl.pallas_call(
        route_kernel,
        out_shape=(
            jax.ShapeDtypeStruct((32, 8192), BF16),
            jax.ShapeDtypeStruct((64, 128), jnp.int32),
        ),
        in_specs=[VMEM] * 3,
        out_specs=(VMEM, VMEM),
        scratch_shapes=[
            pltpu.VMEM((N_DEV, 16, 128), BF16),
            pltpu.VMEM((N_DEV, 16, 128), BF16),
            pltpu.VMEM((64, 1, 128), jnp.int32),
            pltpu.VMEM((N_DEV, 1, 128), jnp.int32),
            pltpu.SemaphoreType.DMA((2,)),
            pltpu.SemaphoreType.DMA((2,)),
        ],
        compiler_params=pltpu.CompilerParams(collective_id=0, has_side_effects=True),
        name="route",
    )(feats, ids, counts)


def tag_rows(tags_ref, step):
    block = tags_ref[pl.ds(pl.multiple_of(step * 8, 8), 8), :]
    tags = jnp.concatenate([block[j : j + 1] for j in range(8)], axis=1)
    along = tags & 255
    lane = (along >> 1) + (along & 1) * 128
    picks = jnp.where(iota((256, CHUNK), 0) == lane, 1.0, 0.0).astype(BF16)
    return tags >> 8, picks


def scatter_kernel(x_ref, tags_ref, active_ref, grid_ref, mask_ref, total):
    total[...] = jnp.zeros_like(total)

    def body(step, carry):
        column, picks = tag_rows(tags_ref, step)
        x = x_ref[:, pl.ds(pl.multiple_of(step * CHUNK, CHUNK), CHUNK)].astype(F32)
        spread = jnp.concatenate(
            [jnp.where(column == v, x, 0.0).astype(BF16) for v in range(16)], axis=0
        )
        total[...] += lax.dot_general(spread, picks, NT, preferred_element_type=F32)
        return carry

    lax.fori_loop(0, 8192 // CHUNK, body, 0)
    z = iota((256, 256), 0)
    order = jnp.where((z >> 1) + (z & 1) * 128 == iota((256, 256), 1), 1.0, 0.0)
    mask = jnp.dot(
        active_ref[...].astype(F32).astype(BF16), order.astype(BF16), preferred_element_type=F32
    )
    mask_ref[...] = mask
    for v in range(16):
        grid_ref[v // 4, v % 4] = (total[32 * v : 32 * v + 32, :] * mask[v : v + 1]).astype(BF16)


def scatter(x, tags, active):
    return pl.pallas_call(
        scatter_kernel,
        out_shape=(
            jax.ShapeDtypeStruct((4, 4, 32, 256), BF16),
            jax.ShapeDtypeStruct((16, 256), F32),
        ),
        in_specs=[VMEM] * 3,
        out_specs=(VMEM, VMEM),
        scratch_shapes=[pltpu.VMEM((512, 256), F32)],
        name="scatter",
    )(x, tags, active)


SHIFTS = [(a, b, c) for a in (0, 1, -1) for b in (0, 1, -1) for c in (0, 1, -1)][1:]


COLUMN = [(0, 0, c) for c in range(1, GZ)]
PLANE = [(a, b, 0) for a in range(GX) for b in range(GY)][1:]
PARTNERS = SHIFTS + [(0, 0, c) for c in range(2, GZ - 1)] + [s for s in PLANE if 2 in s]


def near(ix, iy, iz, shift):
    return flat_id(
        lax.rem(ix + shift[0] + GX, GX),
        lax.rem(iy + shift[1] + GY, GY),
        lax.rem(iz + shift[2] + GZ, GZ),
    )


FROM = {0: pl.ds(1, 4), 1: pl.ds(4, 1), -1: pl.ds(1, 1)}
INTO = {0: pl.ds(1, 4), 1: pl.ds(0, 1), -1: pl.ds(5, 1)}


def halo_start(cells, before, after, send_sem, recv_sem):
    ix, iy, iz = place()
    for shift in SHIFTS:
        a, b, c = shift
        to = near(ix, iy, iz, shift)
        if c == 0:
            src, dst, k = cells.at[FROM[a], FROM[b]], cells.at[INTO[a], INTO[b]], 0
        elif c == 1:
            src = cells.at[FROM[a], FROM[b], :, pl.ds(128, 128)]
            dst, k = before.at[INTO[a], INTO[b]], 1
        else:
            src = cells.at[FROM[a], FROM[b], :, pl.ds(0, 128)]
            dst, k = after.at[INTO[a], INTO[b]], 2
        send(src, dst, send_sem.at[k], recv_sem.at[k], to)


def halo_drain(cells, before, after, sems):
    drain(cells.at[pl.ds(0, 5), pl.ds(0, 4)], sems.at[0])
    drain(before, sems.at[1])
    drain(after, sems.at[2])


def halo_finish(cells, before, after, recv_sem, stack):
    ix, iy, iz = place()
    halo_drain(cells, before, after, recv_sem)
    chan = cells.shape[2]
    for index, axis_len, at in ((ix, GX, 0), (iy, GY, 1)):
        for edge, outside in ((0, 0), (axis_len - 1, 5)):

            @pl.when(index == edge)
            def _():
                for ref in (cells, before, after):
                    for k in range(6):
                        spot = (outside, k) if at == 0 else (k, outside)
                        ref[spot] = jnp.zeros(ref.shape[2:], BF16)

    @pl.when(iz == 0)
    def _():
        before[...] = jnp.zeros(before.shape, BF16)

    @pl.when(iz == GZ - 1)
    def _():
        after[...] = jnp.zeros(after.shape, BF16)

    lane = iota((chan, 128), 1)

    def body(v, carry):
        x, y = lax.div(v, 6), lax.rem(v, 6)
        even = cells[x, y, :, 0:128]
        odd = cells[x, y, :, 128:256]
        prev = jnp.where(lane == 127, before[x, y].astype(F32), odd.astype(F32))
        nxt = jnp.where(lane == 0, after[x, y].astype(F32), even.astype(F32))
        stack[v, 0:chan, 0:128] = pltpu.roll(prev, 1, 1).astype(BF16)
        stack[v, 0:chan, 128:256] = even
        stack[v, chan : 2 * chan, 0:128] = even
        stack[v, chan : 2 * chan, 128:256] = odd
        stack[v, 2 * chan : 3 * chan, 0:128] = odd
        stack[v, 2 * chan : 3 * chan, 128:256] = pltpu.roll(nxt, 127, 1).astype(BF16)
        return carry

    lax.fori_loop(0, 36, body, 0)


def patches(stack, v):
    p, q = lax.div(v, 4), lax.rem(v, 4)
    rows = 3 * stack.shape[1]
    return jnp.concatenate(
        [stack[pl.ds((p + a) * 6 + q, 3)].reshape(rows, 256) for a in range(3)], axis=0
    )


def to_row(partial):
    wide = jnp.concatenate([partial, jnp.zeros_like(partial)], axis=0)
    return jnp.sum(wide.T, axis=0, keepdims=True)


def to_col(row):
    row = row[:, :64]
    same = iota((64, 64), 0) == iota((64, 64), 1)
    return jnp.sum(jnp.where(same, row, 0.0), axis=1, keepdims=True)


def tile_of(rows):
    sub = iota((8, 128), 0)
    out = jnp.zeros((8, 128), F32)
    for k, row in enumerate(rows):
        out = jnp.where(sub == k, row, out)
    return out


def all_combine(tile, combine, z_buf, xy_buf, send_sem, recv_sem):
    ix, iy, iz = place()
    mine = ix * GY + iy
    z_buf[iz] = tile
    for shift in COLUMN:
        to = near(ix, iy, iz, shift)
        send(z_buf.at[iz], z_buf.at[iz], send_sem.at[0], recv_sem.at[0], to)
    drain(z_buf.at[pl.ds(0, GZ - 1)], recv_sem.at[0])
    xy_buf[mine] = combine([z_buf[k] for k in range(GZ)])
    for shift in PLANE:
        to = near(ix, iy, iz, shift)
        send(xy_buf.at[mine], xy_buf.at[mine], send_sem.at[1], recv_sem.at[1], to)
    drain(xy_buf.at[pl.ds(0, N_XY - 1)], recv_sem.at[1])
    out = combine([xy_buf[k] for k in range(N_XY)])
    drain(z_buf.at[pl.ds(0, GZ - 1)], send_sem.at[0])
    drain(xy_buf.at[pl.ds(0, N_XY - 1)], send_sem.at[1])
    return out


def add_tiles(tiles):
    while len(tiles) > 1:
        tiles = [tiles[k] + tiles[k + 1] for k in range(0, len(tiles), 2)]
    return tiles[0]


def merge_moments(tiles):
    whole = add_tiles(tiles)
    mean = whole[0:1] / jnp.maximum(whole[2:3], 1.0)
    square = jnp.zeros((1, 128), F32)
    for t in tiles:
        gap = t[0:1] / jnp.maximum(t[2:3], 1.0) - mean
        square = square + (t[1:2] + t[2:3] * gap * gap)
    return tile_of([whole[0:1], square, whole[2:3]])


def fold(block):
    return block[:, :128] + block[:, 128:]


def core_kernel(
    grid_ref, mask_ref, w_sub_ref, w_back_ref, w_down_ref, w_down_t_ref, gain_ref, shift_ref, ct_ref,
    coarse_ref, back_ref, sub_ref, down_ref, stats_ref,
    cells, before, after, stack, hid, fine, g_fine, g_cells, g_before, g_after, g_stack, gc_all,
    z_one, xy_one, z_two, xy_two, sub_acc,
    halo_send, halo_recv, g_send, g_recv, one_send, one_recv, two_send, two_recv,
):
    ix, iy, iz = place()
    barrier = pltpu.get_barrier_semaphore()
    for shift in PARTNERS:
        pl.semaphore_signal(barrier, inc=1, device_id=near(ix, iy, iz, shift), device_id_type=LOGICAL)
    for v in range(16):
        cells[1 + v // 4, 1 + v % 4] = grid_ref[v // 4, v % 4]
    pl.semaphore_wait(barrier, len(PARTNERS))
    halo_start(cells, before, after, halo_send, halo_recv)

    coarse_masks = []
    for u in range(4):
        up, uq = u // 2, u % 2
        seen = jnp.zeros((1, 128), F32)
        for a in range(2):
            for b in range(2):
                v = (2 * up + a) * 4 + 2 * uq + b
                seen = jnp.maximum(seen, mask_ref[v : v + 1, 0:128])
                seen = jnp.maximum(seen, mask_ref[v : v + 1, 128:256])
        coarse_masks.append(seen)
        grad_c = (ct_ref[:, 128 * u : 128 * u + 128].astype(F32) * seen).astype(BF16)
        gc_all[:, 128 * u : 128 * u + 128] = grad_c
        pulled = jnp.dot(w_down_t_ref[...], grad_c, preferred_element_type=F32)
        for a in range(2):
            for b in range(2):
                for c in range(2):
                    at = ((a * 2 + b) * 2 + c) * 64
                    v = (2 * up + a) * 4 + 2 * uq + b
                    g_fine[v, :, 128 * c : 128 * c + 128] = pulled[at : at + 64]

    halo_finish(cells, before, after, halo_recv, stack)

    def conv(v, total):
        out = jnp.dot(w_sub_ref[...], patches(stack, v), preferred_element_type=F32)
        out = out * mask_ref[pl.ds(v, 1), :]
        hid[v] = out
        return total + fold(out)

    total = lax.fori_loop(0, 16, conv, jnp.zeros((64, 128), F32))
    count = jnp.sum(jnp.sum(mask_ref[...], axis=0, keepdims=True), axis=1, keepdims=True)
    own_mean = jnp.sum(total, axis=1, keepdims=True) / jnp.maximum(count, 1.0)

    def spread(v, acc):
        gap = (hid[v] - own_mean) * mask_ref[pl.ds(v, 1), :]
        return acc + fold(gap * gap)

    square = lax.fori_loop(0, 16, spread, jnp.zeros((64, 128), F32))
    count_row = jnp.broadcast_to(count, (1, 128))
    merged = all_combine(
        tile_of([to_row(total), to_row(square), count_row]), merge_moments, z_one, xy_one, one_send, one_recv
    )
    n_active = merged[2:3]
    mean = to_col(merged[0:1] / n_active)
    inverse = to_col(lax.rsqrt(merged[1:2] / n_active + EPS))
    gain, shift = to_col(gain_ref[...]), to_col(shift_ref[...])

    def norm(v, sums):
        on = mask_ref[pl.ds(v, 1), :]
        normed = (hid[v] - mean) * inverse
        pre = gain * normed + shift
        sq = pre * pre
        bend = jnp.tanh(TANH_SCALE * (pre + TANH_CUBE * (sq * pre)))
        half = 0.5 * (1.0 + bend)
        out = (pre * half * on).astype(BF16)
        p, q = lax.div(v, 4), lax.rem(v, 4)
        at = (lax.rem(p, 2) * 2 + lax.rem(q, 2)) * 2
        u = lax.div(p, 2) * 2 + lax.div(q, 2)
        fine[u, at] = out[:, :128]
        fine[u, at + 1] = out[:, 128:]
        slope = half + pre * (0.5 * TANH_SCALE) * (1.0 - bend * bend) * (1.0 + (3.0 * TANH_CUBE) * sq)
        grad = on * slope * g_fine[v]
        g_fine[v] = grad
        return sums[0] + fold(grad), sums[1] + fold(grad * normed)

    zero = jnp.zeros((64, 128), F32)
    sum_shift, sum_gain = lax.fori_loop(0, 16, norm, (zero, zero))
    sums = all_combine(
        tile_of([to_row(sum_shift), to_row(sum_gain)]), add_tiles, z_two, xy_two, two_send, two_recv
    )
    stats_ref[...] = tile_of([sums[0:1], sums[1:2], n_active])
    mean_shift, mean_gain = to_col(sums[0:1] / n_active), to_col(sums[1:2] / n_active)
    factor = gain * inverse

    def hidden_grad(v, carry):
        normed = (hid[v] - mean) * inverse
        out = mask_ref[pl.ds(v, 1), :] * factor * (g_fine[v] - (mean_shift + normed * mean_gain))
        g_cells[1 + lax.div(v, 4), 1 + lax.rem(v, 4)] = out.astype(BF16)
        return carry

    lax.fori_loop(0, 16, hidden_grad, 0)
    halo_start(g_cells, g_before, g_after, g_send, g_recv)

    down = jnp.zeros((64, 512), F32)
    for u in range(4):
        block = fine[u].reshape(512, 128)
        out = jnp.dot(w_down_ref[...], block, preferred_element_type=F32) * coarse_masks[u]
        coarse_ref[:, 128 * u : 128 * u + 128] = out.astype(BF16)
        down = down + lax.dot_general(
            gc_all[:, 128 * u : 128 * u + 128], block, NT, preferred_element_type=F32
        )
    down_ref[...] = down
    sub_acc[...] = jnp.zeros_like(sub_acc)

    def weigh(v, carry):
        grad = g_cells[1 + lax.div(v, 4), 1 + lax.rem(v, 4)]
        sub_acc[...] += lax.dot_general(patches(stack, v), grad, NT, preferred_element_type=F32)
        return carry

    lax.fori_loop(0, 16, weigh, 0)
    sub_ref[...] = sub_acc[...].T

    halo_finish(g_cells, g_before, g_after, g_recv, g_stack)

    def back(v, carry):
        out = jnp.dot(w_back_ref[...], patches(g_stack, v), preferred_element_type=F32)
        back_ref[v] = (out * mask_ref[pl.ds(v, 1), :]).astype(BF16)
        return carry

    lax.fori_loop(0, 16, back, 0)
    halo_drain(cells, before, after, halo_send)
    halo_drain(g_cells, g_before, g_after, g_send)


def core(grid, mask, w_sub, w_back, w_down, w_down_t, gain, shift, ct):
    dma = pltpu.SemaphoreType.DMA
    return pl.pallas_call(
        core_kernel,
        out_shape=(
            jax.ShapeDtypeStruct((64, 512), BF16),
            jax.ShapeDtypeStruct((16, 32, 256), BF16),
            jax.ShapeDtypeStruct((64, 864), F32),
            jax.ShapeDtypeStruct((64, 512), F32),
            jax.ShapeDtypeStruct((8, 128), F32),
        ),
        in_specs=[VMEM] * 9,
        out_specs=(VMEM,) * 5,
        scratch_shapes=[
            pltpu.VMEM((6, 6, 32, 256), BF16),
            pltpu.VMEM((6, 6, 32, 128), BF16),
            pltpu.VMEM((6, 6, 32, 128), BF16),
            pltpu.VMEM((36, 96, 256), BF16),
            pltpu.VMEM((16, 64, 256), F32),
            pltpu.VMEM((4, 8, 64, 128), BF16),
            pltpu.VMEM((16, 64, 256), F32),
            pltpu.VMEM((6, 6, 64, 256), BF16),
            pltpu.VMEM((6, 6, 64, 128), BF16),
            pltpu.VMEM((6, 6, 64, 128), BF16),
            pltpu.VMEM((36, 192, 256), BF16),
            pltpu.VMEM((64, 512), BF16),
            pltpu.VMEM((GZ, 8, 128), F32),
            pltpu.VMEM((N_XY, 8, 128), F32),
            pltpu.VMEM((GZ, 8, 128), F32),
            pltpu.VMEM((N_XY, 8, 128), F32),
            pltpu.VMEM((864, 64), F32),
            dma((3,)), dma((3,)), dma((3,)), dma((3,)), dma((2,)), dma((2,)), dma((2,)), dma((2,)),
        ],
        compiler_params=pltpu.CompilerParams(collective_id=1, has_side_effects=True),
        name="core",
    )(grid, mask, w_sub, w_back, w_down, w_down_t, gain, shift, ct)


def gather_kernel(back_ref, tags_ref, out_ref):
    def body(step, carry):
        column, picks = tag_rows(tags_ref, step)
        values = jnp.dot(back_ref[...].reshape(512, 256), picks, preferred_element_type=F32)
        out = jnp.zeros((32, CHUNK), F32)
        for v in range(16):
            out = jnp.where(column == v, values[32 * v : 32 * v + 32], out)
        out = out.astype(BF16)
        for j in range(8):
            block = out[:, 128 * j : 128 * j + 128]
            first, second = halves(block[:16], block[16:])
            out_ref[step * 16 + 2 * j] = first
            out_ref[step * 16 + 2 * j + 1] = second
        return carry

    lax.fori_loop(0, 8192 // CHUNK, body, 0)


def gather(back, tags):
    return pl.pallas_call(
        gather_kernel,
        out_shape=jax.ShapeDtypeStruct((N_DEV, 16, 128), BF16),
        in_specs=[VMEM] * 2,
        out_specs=VMEM,
        name="gather",
    )(back, tags)


TILES = 11


def home_kernel(
    slots_ref, sub_ref, down_ref, stats_ref, points_ref, sub_out, down_out,
    in_buf, w_out, w_in, p_out, p_in, f_buf, a_buf, send_sem, recv_sem,
):
    ix, iy, iz = place()
    me = flat_id(ix, iy, iz)
    mine = ix * GY + iy
    barrier = pltpu.get_barrier_semaphore()
    greet_all(me, barrier)
    for k in range(GZ):
        rows = slice(8 * k, 8 * k + 8)
        for t in range(6):
            w_out[k, t] = sub_ref[rows, 128 * t : 128 * t + 128]
        w_out[k, 6] = jnp.concatenate([sub_ref[rows, 768:864], jnp.zeros((8, 32), F32)], axis=1)
        for t in range(4):
            w_out[k, 7 + t] = down_ref[rows, 128 * t : 128 * t + 128]
    for t in range(TILES, N_XY):
        p_out[t] = jnp.zeros((8, 128), F32)
    pl.semaphore_wait(barrier, N_DEV - 1)

    for shift in COLUMN:
        z = lax.rem(iz + shift[2] + GZ, GZ)
        to = near(ix, iy, iz, shift)
        send(w_out.at[z], w_in.at[iz], send_sem.at[1], recv_sem.at[1], to)

    def go(step, carry):
        to = lax.rem(me + step, N_DEV)
        send(slots_ref.at[to], in_buf.at[me], send_sem.at[0], recv_sem.at[0], to)
        return carry

    lax.fori_loop(1, N_DEV, go, 0)
    in_buf[me] = slots_ref[me]
    w_in[iz] = w_out[iz]
    drain(w_in.at[pl.ds(0, GZ - 1)], recv_sem.at[1])
    for t in range(TILES):
        p_out[t] = add_tiles([w_in[k, t] for k in range(GZ)])
    for shift in PLANE:
        other = lax.rem(ix + shift[0] + GX, GX) * GY + lax.rem(iy + shift[1] + GY, GY)
        to = near(ix, iy, iz, shift)
        send(p_out.at[other], p_in.at[mine], send_sem.at[2], recv_sem.at[2], to)
    p_in[mine] = p_out[mine]
    drain(p_in.at[pl.ds(0, N_XY - 1)], recv_sem.at[2])
    scale = lax.rsqrt(stats_ref[2:3, :])
    f_buf[mine] = add_tiles([p_in[k] for k in range(N_XY)]) * scale
    for shift in PLANE:
        to = near(ix, iy, iz, shift)
        send(f_buf.at[mine], f_buf.at[mine], send_sem.at[3], recv_sem.at[3], to)
    drain(f_buf.at[pl.ds(0, N_XY - 1)], recv_sem.at[3])
    whole = f_buf.at[pl.ds(0, TILES)]
    for shift in COLUMN:
        to = near(ix, iy, iz, shift)
        send(whole, a_buf.at[iz], send_sem.at[4], recv_sem.at[4], to)
    for t in range(TILES):
        a_buf[iz, t] = f_buf[t]
    drain(in_buf.at[pl.ds(0, N_DEV - 1)], recv_sem.at[0])

    def unpack(m, carry):
        top, bottom = halves(in_buf[2 * m], in_buf[2 * m + 1])
        at = pl.ds(pl.multiple_of(m * 128, 128), 128)
        points_ref[0:16, at] = top
        points_ref[16:32, at] = bottom
        return carry

    lax.fori_loop(0, 64, unpack, 0)
    drain(a_buf.at[pl.ds(0, GZ - 1)], recv_sem.at[4])
    for k in range(GZ):
        rows = slice(8 * k, 8 * k + 8)
        for t in range(6):
            sub_out[rows, 128 * t : 128 * t + 128] = a_buf[k, t]
        sub_out[rows, 768:864] = a_buf[k, 6][:, :96]
        for t in range(4):
            down_out[rows, 128 * t : 128 * t + 128] = a_buf[k, 7 + t]
    drain(in_buf.at[pl.ds(0, N_DEV - 1)], send_sem.at[0])
    drain(w_in.at[pl.ds(0, GZ - 1)], send_sem.at[1])
    drain(p_in.at[pl.ds(0, N_XY - 1)], send_sem.at[2])
    drain(f_buf.at[pl.ds(0, N_XY - 1)], send_sem.at[3])
    drain(a_buf.at[pl.ds(0, GZ - 1)], send_sem.at[4])


def home(slots, sub, down, stats):
    return pl.pallas_call(
        home_kernel,
        out_shape=(
            jax.ShapeDtypeStruct((32, 8192), BF16),
            jax.ShapeDtypeStruct((64, 864), F32),
            jax.ShapeDtypeStruct((64, 512), F32),
        ),
        in_specs=[VMEM] * 4,
        out_specs=(VMEM,) * 3,
        scratch_shapes=[
            pltpu.VMEM((N_DEV, 16, 128), BF16),
            pltpu.VMEM((GZ, TILES, 8, 128), F32),
            pltpu.VMEM((GZ, TILES, 8, 128), F32),
            pltpu.VMEM((N_XY, 8, 128), F32),
            pltpu.VMEM((N_XY, 8, 128), F32),
            pltpu.VMEM((N_XY, 8, 128), F32),
            pltpu.VMEM((GZ, TILES, 8, 128), F32),
            pltpu.SemaphoreType.DMA((5,)),
            pltpu.SemaphoreType.DMA((5,)),
        ],
        compiler_params=pltpu.CompilerParams(collective_id=2, has_side_effects=True),
        name="home",
    )(slots, sub, down, stats)


def on_device(
    point_feats, voxel_ids, send_counts, active, w_sub, w_down, bn_gain, bn_shift, cotangent
):
    x, tags = route(point_feats, voxel_ids.reshape(64, 128), send_counts)
    grid, mask = scatter(x, tags, active.reshape(16, 256))
    w_back = w_sub.reshape(64, 3, 3, 3, 32)[:, ::-1, ::-1, ::-1].transpose(4, 1, 2, 3, 0)
    coarse, back, sub, down, stats = core(
        grid,
        mask,
        w_sub,
        w_back.reshape(32, 27 * 64),
        w_down,
        w_down.T,
        bn_gain.reshape(1, 64),
        bn_shift.reshape(1, 64),
        cotangent.reshape(64, 512),
    )
    points, grad_sub, grad_down = home(gather(back, tags), sub, down, stats)
    scale = lax.rsqrt(stats[2, :64])
    return (
        coarse.reshape(64, 2, 2, 128),
        points,
        grad_sub,
        grad_down,
        stats[1, :64] * scale,
        stats[0, :64] * scale,
    )


def solution(mesh):
    every = ("gx", "gy", "gz")
    in_specs = (
        P(None, every), P(every), P(every, None), P(*every),
        P(), P(), P(), P(), P(None, *every),
    )
    out_specs = (P(None, *every), P(None, every), P(), P(), P(), P())
    return jax.shard_map(
        on_device, mesh=mesh, in_specs=in_specs, out_specs=out_specs, check_vma=False
    )
```

time: 591 us -> 144 us (0.24); the launches traced: 583 us -> 143 us
  blocking collectives: 189 us -> 0 us
  local copies, waits for them, and re-layouts: 158 us -> 8.38 us
  Pallas kernels: 0 us -> 133 us
  other arithmetic: 99.2 us -> 1.31 us
  starting transfers between devices: 57.1 us -> 0 us
  waiting for transfers between devices: 39.4 us -> 0 us
  matrix products: 23.5 us -> 0 us
  between operations: 16.3 us -> 0.71 us
    psum x3 -> x0, blocking collectives: 189 us -> none  [the longest x1 63.5 us: on_device(): lax.psum((jnp.sum(grad_pre, axis=1), jnp.sum(grad_pre * normed, axis=1)),...]
    pallas_call x0 -> x5, Pallas kernels: none -> 133 us  [the longest x1 58.2 us: core(): pl.pallas_call(core_kernel, out_shape=(jax.ShapeDtypeStruct((64, 512), BF...]
    reshape x34 -> x4, local copies, waits for them, and re-layouts: 56 us -> 3.62 us  [the longest x1 1.49 us: on_device(): coarse.reshape(64, 2, 2, 128)]
    scatter-add x1 -> x0, other arithmetic: 50.6 us -> none  [on_device(): jax.ops.segment_sum(arriving.T.astype(jnp.float32), target, num_segments=...]
    concatenate x18 -> x0, other arithmetic: 30.8 us -> none  [the longest x12 21.5 us: columns(): joined = jnp.concatenate(pieces, axis=0)]
    ppermute x12 -> x0, starting transfers between devices: 29.4 us -> none  [the longest x6 19.7 us: padded_2(): lax.ppermute(tail, axis, [(i, (i + 1) % count) for i in range(ends)])]
    concatenate x15 -> x0, local copies, waits for them, and re-layouts: 29 us -> none  [the longest x12 28.2 us: columns(): joined = jnp.concatenate(pieces, axis=0)]
    all_to_all x3 -> x0, starting transfers between devices: 27.3 us -> none  [the longest x1 11.5 us: on_device(): lax.all_to_all(voxel_tags, ('gx', 'gy', 'gz'), split_axis=1, concat_axis=...]
  transfers between devices with their start and end apart: 16 -> 0, of which waited for: 10 -> 0; matrix products, arithmetic and copies ran while one was open for 25% -> 0% of each run, Pallas kernels for 0% -> 0%
where the time goes in v1:
time: 144 us; the launch traced here: 143 us
  Pallas kernels  133 us (92%)
  local copies, waits for them, and re-layouts  8.38 us (6%)
    pallas_call x1, Pallas kernels, core(): pl.pallas_call(core_kernel, out_shape=(jax.ShapeDtypeStruct((64, 512), BF...  58.2 us
    pallas_call x1, Pallas kernels, home(): pl.pallas_call(home_kernel, out_shape=(jax.ShapeDtypeStruct((32, 8192), B...  34.4 us
    pallas_call x1, Pallas kernels, route(): pl.pallas_call(route_kernel, out_shape=(jax.ShapeDtypeStruct((32, 8192),...  28.4 us
    pallas_call x1, Pallas kernels, gather(): pl.pallas_call(gather_kernel, out_shape=jax.ShapeDtypeStruct((N_DEV, 16,...  5.94 us
    pallas_call x1, Pallas kernels, scatter(): pl.pallas_call(scatter_kernel, out_shape=(jax.ShapeDtypeStruct((4, 4, 32,...  5.92 us
    unnamed x17, local copies, waits for them, and re-layouts  4.58 us

profile of v1, /device:TPU:1, one launch (start us, length us, event | category | flops | bytes accessed | tf_op | source)
XLA Modules:
  0.0 143.3 jit_solution(13368666069681830650)
XLA Ops:
  0.6 0.0 copy-start.5
  0.6 28.4 %route.1 = (bf16[32,8192]{1,0:T(8,128)(2,1)}, s32[64,128]{1,0:T(8,128)}) custom-call(bf16[32,8192]{1,0:T(8,128)(2,1)} %feats_ref.1, s32[64,128]{1,0:T(8,128)} %bitcast.13, s32[1,128]{1,0:T(1,128)} %counts_ref.1), custom_call_target="tpu_custom_call" | custom-call | tf_op jit(solution)/shard_map/route/pallas_call | solution.py:126
  29.1 0.0 copy-done.5
  29.1 0.6 reshape.40.active_ref
  29.7 0.0 copy-start
  29.7 5.9 %scatter.1 = (bf16[4,4,32,256]{3,2,1,0:T(8,128)(2,1)}, f32[16,256]{1,0:T(8,128)}) custom-call(bf16[32,8192]{1,0:T(8,128)(2,1)} %get-tuple-element.18.x_ref, s32[64,128]{1,0:T(8,128)} %get-tuple-element.19.tags_ref, s32[16,256]{1,0:T(8,128)} %reshape.40.active_ref), custom_call_target="tpu_custom_call" | custom-call | tf_op jit(solution)/shard_map/scatter/pallas_call | solution.py:180
  35.6 0.0 copy-done
  35.6 0.2 copy.17
  35.8 0.2 copy.18
  36.0 0.0 copy-start.1
  36.0 0.9 reshape.42.w_back_ref
  36.8 0.0 copy-done.1
  36.8 0.0 copy-start.4
  36.8 0.8 copy.19
  37.6 0.1 copy-done.4
  37.7 0.7 reshape.45.ct_ref
  38.3 58.2 %core.1 = (bf16[64,512]{1,0:T(8,128)(2,1)}, bf16[16,32,256]{2,1,0:T(8,128)(2,1)}, f32[64,864]{1,0:T(8,128)}, f32[64,512]{1,0:T(8,128)}, f32[8,128]{1,0:T(8,128)}) custom-call(bf16[4,4,32,256]{3,2,1,0:T(8,128)(2,1)} %get-tuple-element.20.grid_ref, f32[16,256]{1,0:T(8,128)} %get-tuple-element.21.mask_ref, bf16[64,864]{1,0:T(8,128)(2,1)} %w_sub_ref.1, ...), custom_call_target="tpu_custom_call" | custom-call | tf_op jit(solution)/shard_map/core/pallas_call | solution.py:473
  96.6 1.5 %reshape.46 = bf16[64,2,2,128]{3,2,1,0:T(2,128)(2,1)} reshape(bf16[64,512]{1,0:T(8,128)(2,1)} %get-tuple-element.22) | data formatting | bytes 131072 | tf_op jit(solution)/shard_map/reshape | solution.py:665
  98.1 5.9 %gather.1.slots_ref = bf16[128,16,128]{2,1,0:T(8,128)(2,1)} custom-call(bf16[16,32,256]{2,1,0:T(8,128)(2,1)} %get-tuple-element.23.back_ref, s32[64,128]{1,0:T(8,128)} %get-tuple-element.19.tags_ref), custom_call_target="tpu_custom_call" | custom-call | tf_op jit(solution)/shard_map/gather/pallas_call | solution.py:528
  104.0 34.4 %home.1 = (bf16[32,8192]{1,0:T(8,128)(2,1)}, f32[64,864]{1,0:T(8,128)}, f32[64,512]{1,0:T(8,128)}) custom-call(bf16[128,16,128]{2,1,0:T(8,128)(2,1)} %gather.1.slots_ref, f32[64,864]{1,0:T(8,128)} %get-tuple-element.24.sub_ref, f32[64,512]{1,0:T(8,128)} %get-tuple-element.25.down_ref, f32[8,128]{1,0:T(8,128)} %get-tuple-element.26.stats_ref), custom_call_target="tpu_custom_call" | custom-call | tf_op jit(solution)/shard_map/home/pallas_call | solution.py:620
  138.5 1.3 multiply_bitcast_fusion
  139.8 0.0 copy-start.2
  139.8 1.9 %copy.23 = bf16[32,8192]{1,0:T(8,128)(2,1)} copy(bf16[32,8192]{1,0:T(8,128)(2,1)} %get-tuple-element.39) | data formatting | bytes 1048576
  141.7 0.0 copy-done.2
  141.7 0.0 copy-start.3
  141.7 0.7 copy.24
  142.4 0.3 copy-done.3
  142.7 0.7 copy.25
  (1 shorter events, 0.0 us)
Async XLA Ops:
  0.6 28.4 %copy-start.5 = (s32[4,4,256]{2,1,0:T(4,128)S(1)}, s32[4,4,256]{2,1,0:T(4,128)}, u32[]{:S(2)}) copy-start(s32[4,4,256]{2,1,0:T(4,128)} %param.12) | copy-start | bytes 49156
  29.7 5.9 %copy-start = (bf16[64,864]{1,0:T(8,128)(2,1)S(1)}, bf16[64,864]{1,0:T(8,128)(2,1)}, u32[]{:S(2)}) copy-start(bf16[64,864]{1,0:T(8,128)(2,1)} %w_sub_ref.1) | copy-start | bytes 331780
  36.0 0.9 copy-start.1
  36.8 0.8 copy-start.4
  139.8 1.9 %copy-start.2 = (f32[64,864]{1,0:T(8,128)S(1)}, f32[64,864]{1,0:T(8,128)}, u32[]{:S(2)}) copy-start(f32[64,864]{1,0:T(8,128)} %get-tuple-element.40) | copy-start | bytes 663556
  141.7 1.0 copy-start.3

commit v2 on v0

v2 whole, which is shorter than its diff:
```python
import jax
import jax.numpy as jnp
from jax import lax
from jax.experimental import pallas as pl
from jax.experimental.pallas import tpu as pltpu
from jax.sharding import PartitionSpec as P

EPS = 1e-05
TANH_SCALE = 0.7978845608028654
TANH_CUBE = 0.044715
F32 = jnp.float32
BF16 = jnp.bfloat16
LOGICAL = pl.DeviceIdType.LOGICAL
VMEM = pl.BlockSpec(memory_space=pltpu.VMEM)
NT = (((1,), (1,)), ((), ()))
TN = (((0,), (0,)), ((), ()))
GX, GY, GZ = 4, 4, 8
N_DEV = GX * GY * GZ
N_XY = GX * GY
GROUP = 16
N_GROUP = N_DEV // GROUP
CHUNK = GROUP * 64
TILES = 11
COLUMN = [(0, 0, c) for c in range(1, GZ)]
PLANE = [(a, b, 0) for a in range(GX) for b in range(GY)][1:]
SIDES = [(a, b, 0) for a in (0, 1, -1) for b in (0, 1, -1)][1:]


def iota(shape, dim):
    return lax.broadcasted_iota(jnp.int32, shape, dim)


class Place:
    def __init__(self):
        self.x, self.y, self.z = (lax.axis_index(a) for a in ("gx", "gy", "gz"))
        self.xs = {a: lax.rem(self.x + a + GX, GX) for a in range(-1, GX)}
        self.ys = {b: lax.rem(self.y + b + GY, GY) for b in range(-1, GY)}
        self.zs = {c: lax.rem(self.z + c + GZ, GZ) for c in range(-1, GZ)}
        self.plane = self.x * GY + self.y
        self.me = self.plane * GZ + self.z

    def plane_at(self, shift):
        return self.xs[shift[0]] * GY + self.ys[shift[1]]

    def at(self, shift):
        return self.plane_at(shift) * GZ + self.zs[shift[2]]


def drain(ref, sem):
    pltpu.make_async_copy(ref, ref, sem).wait()


def send(src, dst, send_sem, recv_sem, device):
    pltpu.make_async_remote_copy(
        src_ref=src,
        dst_ref=dst,
        send_sem=send_sem,
        recv_sem=recv_sem,
        device_id=device,
        device_id_type=LOGICAL,
    ).start()


def halves(first, second):
    return jnp.concatenate([first[:, :64], second[:, :64]], axis=1), jnp.concatenate(
        [first[:, 64:], second[:, 64:]], axis=1
    )


def one_hot(tags):
    along = tags & 255
    lane = (along >> 1) + (along & 1) * 128
    return jnp.where(iota((256, CHUNK), 0) == lane, 1.0, 0.0).astype(BF16)


FROM = {0: pl.ds(1, 4), 1: pl.ds(4, 1), -1: pl.ds(1, 1)}
INTO = {0: pl.ds(1, 4), 1: pl.ds(0, 1), -1: pl.ds(5, 1)}


def halo_start(here, cells, ends, ends_in, send_sem, recv_sem):
    chan = cells.shape[2]
    for k, half, edge in ((0, 0, 0), (1, 128, 127)):
        faces = jnp.concatenate(
            [cells[1 + v // 4, 1 + v % 4, :, half : half + 128] for v in range(16)], axis=0
        )
        pick = jnp.where(iota((8, 128), 1) == edge, 1.0, 0.0).astype(BF16)
        ends[k] = lax.dot_general(pick, faces, NT, preferred_element_type=F32)[0:1]
    for shift in SIDES:
        a, b, _ = shift
        src, dst = cells.at[FROM[a], FROM[b]], cells.at[INTO[a], INTO[b]]
        send(src, dst, send_sem.at[0], recv_sem.at[0], here.at(shift))
    for k, c in ((0, -1), (1, 1)):
        for a in (0, 1, -1):
            for b in (0, 1, -1):
                slot = (1 - a) * 3 + (1 - b)
                to = here.at((a, b, c))
                send(ends.at[k], ends_in.at[k, slot], send_sem.at[1], recv_sem.at[1], to)


def halo_drain(cells, ends_in, sems):
    drain(cells.at[pl.ds(0, 5), pl.ds(0, 4)], sems.at[0])
    drain(ends_in, sems.at[1])


def halo_finish(here, cells, ends_in, recv_sem, edges, stack):
    halo_drain(cells, ends_in, recv_sem)
    chan = cells.shape[2]
    for index, last, along_x in ((here.x, GX - 1, True), (here.y, GY - 1, False)):
        for edge, outside in ((0, 0), (last, 5)):

            @pl.when(index == edge)
            def _():
                for k in range(6):
                    spot = (outside, k) if along_x else (k, outside)
                    cells[spot] = jnp.zeros((chan, 256), BF16)

    inside_x = {-1: (here.x > 0).astype(F32), 0: 1.0, 1: (here.x < GX - 1).astype(F32)}
    inside_y = {-1: (here.y > 0).astype(F32), 0: 1.0, 1: (here.y < GY - 1).astype(F32)}
    inside_z = ((here.z < GZ - 1).astype(F32), (here.z > 0).astype(F32))
    for k, lane_at in ((0, 127), (1, 0)):
        rows = []
        for x in range(6):
            sx, p = (-1, 3) if x == 0 else ((1, 0) if x == 5 else (0, x - 1))
            parts = []
            for sy, q, width in ((-1, 3, 1), (0, 0, 4), (1, 0, 1)):
                at = (p * 4 + q) * chan
                part = ends_in[k, (sx + 1) * 3 + sy + 1][:, at : at + width * chan]
                parts.append(part * (inside_z[k] * inside_x[sx] * inside_y[sy]))
            rows.append(jnp.concatenate(parts, axis=1))
        rows += [jnp.zeros((1, 6 * chan), F32)] * 2
        rows = jnp.concatenate(rows, axis=0).astype(BF16)
        lane, row = iota((8, 768), 1), iota((8, 768), 0)
        where = jnp.where(lane == row * 128 + lane_at, 1.0, 0.0).astype(BF16)
        spread = lax.dot_general(rows, where, TN, preferred_element_type=F32)
        for x in range(6):
            for y in range(6):
                edges[k, x * 6 + y] = spread[y * chan : (y + 1) * chan, 128 * x : 128 * x + 128]
    lane = iota((chan, 128), 1)

    def body(v, carry):
        x, y = lax.div(v, 6), lax.rem(v, 6)
        even = cells[x, y, :, 0:128]
        odd = cells[x, y, :, 128:256]
        prev = jnp.where(lane == 0, edges[1, v], pltpu.roll(odd.astype(F32), 1, 1))
        nxt = jnp.where(lane == 127, edges[0, v], pltpu.roll(even.astype(F32), 127, 1))
        stack[v, 0:chan, 0:128] = prev.astype(BF16)
        stack[v, 0:chan, 128:256] = even
        stack[v, chan : 2 * chan, 0:128] = even
        stack[v, chan : 2 * chan, 128:256] = odd
        stack[v, 2 * chan : 3 * chan, 0:128] = odd
        stack[v, 2 * chan : 3 * chan, 128:256] = nxt.astype(BF16)
        return carry

    lax.fori_loop(0, 36, body, 0)


def patches(stack, v):
    p, q = lax.div(v, 4), lax.rem(v, 4)
    rows = 3 * stack.shape[1]
    return jnp.concatenate(
        [stack[pl.ds((p + a) * 6 + q, 3)].reshape(rows, 256) for a in range(3)], axis=0
    )


def to_row(partial):
    wide = jnp.concatenate([partial, jnp.zeros_like(partial)], axis=0)
    return jnp.sum(wide.T, axis=0, keepdims=True)


def to_col(row):
    row = row[:, :64]
    same = iota((64, 64), 0) == iota((64, 64), 1)
    return jnp.sum(jnp.where(same, row, 0.0), axis=1, keepdims=True)


def tile_of(rows):
    sub = iota((8, 128), 0)
    out = jnp.zeros((8, 128), F32)
    for k, row in enumerate(rows):
        out = jnp.where(sub == k, row, out)
    return out


def combine_start(here, tile, bufs):
    z_buf, _, send_sem, recv_sem = bufs
    z_buf[here.z] = tile
    for shift in COLUMN:
        at = z_buf.at[here.z]
        send(at, at, send_sem.at[0], recv_sem.at[0], here.at(shift))


def combine_finish(here, combine, bufs):
    z_buf, xy_buf, send_sem, recv_sem = bufs
    drain(z_buf.at[pl.ds(0, GZ - 1)], recv_sem.at[0])
    xy_buf[here.plane] = combine([z_buf[k] for k in range(GZ)])
    for shift in PLANE:
        at = xy_buf.at[here.plane]
        send(at, at, send_sem.at[1], recv_sem.at[1], here.at(shift))
    drain(xy_buf.at[pl.ds(0, N_XY - 1)], recv_sem.at[1])
    return combine([xy_buf[k] for k in range(N_XY)])


def combine_close(bufs):
    z_buf, xy_buf, send_sem, _ = bufs
    drain(z_buf.at[pl.ds(0, GZ - 1)], send_sem.at[0])
    drain(xy_buf.at[pl.ds(0, N_XY - 1)], send_sem.at[1])


def add_tiles(tiles):
    while len(tiles) > 1:
        tiles = [tiles[k] + tiles[k + 1] for k in range(0, len(tiles), 2)]
    return tiles[0]


def merge_moments(tiles):
    whole = add_tiles(tiles)
    mean = whole[0:1] / jnp.maximum(whole[2:3], 1.0)
    square = jnp.zeros((1, 128), F32)
    for t in tiles:
        gap = t[0:1] / jnp.maximum(t[2:3], 1.0) - mean
        square = square + (t[1:2] + t[2:3] * gap * gap)
    return tile_of([whole[0:1], square, whole[2:3]])


def fold(block):
    return block[:, :128] + block[:, 128:]


def block_kernel(
    feats_ref, ids_ref, counts_ref, active_ref, w_sub_ref, w_down_ref, gain_ref, shift_ref, ct_ref,
    points_ref, coarse_ref, sub_out, down_out, gain_out, shift_out,
    out_buf, in_buf, out_ids, z_ids, all_ids, tag_buf, total, mask_ref, w_back, w_down_t,
    cells, ends, ends_in, edges, stack, hid, fine, g_fine, gc_all,
    g_cells, g_ends, g_ends_in, g_edges, g_stack,
    z_one, xy_one, z_two, xy_two, sub_acc,
    w_out, w_in, p_out, p_in, f_buf, a_buf, home_out, home_in,
    route_send, route_recv, id_send, id_recv, halo_send, halo_recv, g_send, g_recv,
    one_send, one_recv, two_send, two_recv, w_send, w_recv, home_send, home_recv,
):
    here = Place()
    me = here.me
    group = lax.div(me, GROUP)
    member = lax.rem(me, GROUP)
    barrier = pltpu.get_barrier_semaphore()

    def greet(step, carry):
        pl.semaphore_signal(
            barrier, inc=1, device_id=lax.rem(me + step, N_DEV), device_id_type=LOGICAL
        )
        return carry

    lax.fori_loop(1, N_DEV, greet, 0)

    row, lane = iota((64, 128), 0), iota((64, 128), 1)
    counts = counts_ref[...]
    even = jnp.sum(jnp.where(lane == 2 * row, counts, 0), axis=1, keepdims=True)
    odd = jnp.sum(jnp.where(lane == 2 * row + 1, counts, 0), axis=1, keepdims=True)
    usable = (lane & 63) < jnp.where(lane < 64, even, odd)
    tags = jnp.where(usable, ids_ref[...], -1)
    for m in range(64):
        out_ids[m // 4, m % 4] = tags[m : m + 1]

    def pack(m, carry):
        block = feats_ref[:, pl.ds(pl.multiple_of(m * 128, 128), 128)]
        first, second = halves(block[:16], block[16:])
        out_buf[2 * m] = first
        out_buf[2 * m + 1] = second
        return carry

    lax.fori_loop(0, 64, pack, 0)
    pl.semaphore_wait(barrier, N_DEV - 1)

    def go_group(src, dst, sends, recvs, step, first):
        base = lax.rem(group + step, N_GROUP) * GROUP

        def go(t, carry):
            to = base + lax.rem(member + t, GROUP)
            send(src.at[to], dst.at[me], sends.at[0], recvs.at[group], to)
            return carry

        lax.fori_loop(first, GROUP, go, 0)

    for shift in COLUMN:
        k = lax.div(here.zs[shift[2]], 2)
        send(out_ids.at[:, k], z_ids.at[here.z], id_send.at[0], id_recv.at[0], here.at(shift))
    z_ids[here.z] = out_ids[:, lax.div(here.z, 2)]
    keep = pltpu.make_async_copy(out_buf.at[me], in_buf.at[me], route_recv.at[group])
    keep.start()
    go_group(out_buf, in_buf, route_send, route_recv, 0, 1)
    for step in range(1, 4):
        go_group(out_buf, in_buf, route_send, route_recv, step, 0)
    drain(z_ids.at[pl.ds(0, GZ - 1)], id_recv.at[0])
    for shift in PLANE:
        other = here.plane_at(shift)
        send(z_ids.at[:, other], all_ids.at[here.plane], id_send.at[1], id_recv.at[1], here.at(shift))
    all_ids[here.plane] = z_ids[:, here.plane]
    for step in range(4, N_GROUP):
        go_group(out_buf, in_buf, route_send, route_recv, step, 0)

    turned = w_sub_ref[...].astype(F32).T.astype(BF16)
    for e in range(0, 26, 2):
        pair = [turned[32 * (26 - k) : 32 * (27 - k)] for k in (e, e + 1)]
        w_back[:, 64 * e : 64 * e + 128] = jnp.concatenate(pair, axis=1)
    w_back[:, 64 * 26 : 64 * 27] = turned[0:32]
    w_down_t[...] = w_down_ref[...].astype(F32).T.astype(BF16)
    z = iota((256, 256), 0)
    order = jnp.where((z >> 1) + (z & 1) * 128 == iota((256, 256), 1), 1.0, 0.0)
    active = jnp.concatenate([active_ref[p] for p in range(4)], axis=0).astype(F32)
    mask = jnp.dot(active.astype(BF16), order.astype(BF16), preferred_element_type=F32)
    mask_ref[...] = mask
    count = jnp.sum(jnp.sum(mask, axis=0, keepdims=True), axis=1, keepdims=True)

    coarse_masks = []
    for u in range(4):
        up, uq = u // 2, u % 2
        seen = jnp.zeros((1, 128), F32)
        for a in range(2):
            for b in range(2):
                v = (2 * up + a) * 4 + 2 * uq + b
                seen = jnp.maximum(seen, jnp.maximum(mask[v : v + 1, 0:128], mask[v : v + 1, 128:256]))
        coarse_masks.append(seen)
        grad_c = (ct_ref[:, 128 * u : 128 * u + 128].astype(F32) * seen).astype(BF16)
        gc_all[:, 128 * u : 128 * u + 128] = grad_c
        pulled = jnp.dot(w_down_t[...], grad_c, preferred_element_type=F32)
        for a in range(2):
            for b in range(2):
                for c in range(2):
                    at = ((a * 2 + b) * 2 + c) * 64
                    v = (2 * up + a) * 4 + 2 * uq + b
                    g_fine[v, :, 128 * c : 128 * c + 128] = pulled[at : at + 64]

    total[...] = jnp.zeros_like(total)
    low = iota((1, 128), 1) < 64
    first_core = lax.rem(here.z, 2) == 0
    drain(all_ids.at[pl.ds(0, N_XY - 1)], id_recv.at[1])

    def collect(step, carry):
        g = lax.rem(group - step + N_GROUP, N_GROUP)
        drain(in_buf.at[pl.ds(0, GROUP)], route_recv.at[g])
        tops, bottoms, rows = [], [], []
        for t in range(0, GROUP, 2):
            top, bottom = halves(in_buf[g * GROUP + t], in_buf[g * GROUP + t + 1])
            tops.append(top)
            bottoms.append(bottom)
            one, two = (all_ids[g * 2 + k // GZ, k % GZ] for k in (t, t + 1))
            in_first = jnp.where(low, one, pltpu.roll(two, 64, 1))
            in_second = jnp.where(low, pltpu.roll(one, 64, 1), two)
            rows.append(jnp.where(first_core, in_first, in_second))
        tags = jnp.concatenate(rows, axis=1)
        tag_buf[g] = tags
        x = jnp.concatenate(
            [jnp.concatenate(tops, axis=1), jnp.concatenate(bottoms, axis=1)], axis=0
        ).astype(F32)
        column = tags >> 8
        spread = jnp.concatenate(
            [jnp.where(column == v, x, 0.0).astype(BF16) for v in range(16)], axis=0
        )
        total[...] += lax.dot_general(spread, one_hot(tags), NT, preferred_element_type=F32)
        return carry

    lax.fori_loop(0, N_GROUP, collect, 0)
    for v in range(16):
        cells[1 + v // 4, 1 + v % 4] = (total[32 * v : 32 * v + 32, :] * mask[v : v + 1]).astype(BF16)
    halo_start(here, cells, ends, ends_in, halo_send, halo_recv)
    halo_finish(here, cells, ends_in, halo_recv, edges, stack)
    one_bufs = (z_one, xy_one, one_send, one_recv)
    two_bufs = (z_two, xy_two, two_send, two_recv)

    def conv(v, acc):
        out = jnp.dot(w_sub_ref[...], patches(stack, v), preferred_element_type=F32)
        out = out * mask_ref[pl.ds(v, 1), :]
        hid[v] = out
        return acc + fold(out)

    summed = lax.fori_loop(0, 16, conv, jnp.zeros((64, 128), F32))
    own_mean = jnp.sum(summed, axis=1, keepdims=True) / jnp.maximum(count, 1.0)

    def spread(v, acc):
        gap = (hid[v] - own_mean) * mask_ref[pl.ds(v, 1), :]
        return acc + fold(gap * gap)

    square = lax.fori_loop(0, 16, spread, jnp.zeros((64, 128), F32))
    count_row = jnp.broadcast_to(count, (1, 128))
    combine_start(here, tile_of([to_row(summed), to_row(square), count_row]), one_bufs)
    gain, shift = to_col(gain_ref[...]), to_col(shift_ref[...])
    merged = combine_finish(here, merge_moments, one_bufs)
    n_active = merged[2:3]
    mean = to_col(merged[0:1] / n_active)
    inverse = to_col(lax.rsqrt(merged[1:2] / n_active + EPS))

    def norm(v, sums):
        on = mask_ref[pl.ds(v, 1), :]
        normed = (hid[v] - mean) * inverse
        pre = gain * normed + shift
        sq = pre * pre
        bend = jnp.tanh(TANH_SCALE * (pre + TANH_CUBE * (sq * pre)))
        half = 0.5 * (1.0 + bend)
        out = (pre * half * on).astype(BF16)
        p, q = lax.div(v, 4), lax.rem(v, 4)
        at = (lax.rem(p, 2) * 2 + lax.rem(q, 2)) * 2
        u = lax.div(p, 2) * 2 + lax.div(q, 2)
        fine[u, at] = out[:, :128]
        fine[u, at + 1] = out[:, 128:]
        slope = half + pre * (0.5 * TANH_SCALE) * (1.0 - bend * bend) * (1.0 + (3.0 * TANH_CUBE) * sq)
        grad = on * slope * g_fine[v]
        g_fine[v] = grad
        return sums[0] + fold(grad), sums[1] + fold(grad * normed)

    zero = jnp.zeros((64, 128), F32)
    sum_shift, sum_gain = lax.fori_loop(0, 16, norm, (zero, zero))
    combine_start(here, tile_of([to_row(sum_shift), to_row(sum_gain)]), two_bufs)
    down = jnp.zeros((64, 512), F32)
    for u in range(4):
        block = fine[u].reshape(512, 128)
        out = jnp.dot(w_down_ref[...], block, preferred_element_type=F32) * coarse_masks[u]
        coarse_ref[:, 128 * u : 128 * u + 128] = out.astype(BF16)
        down = down + lax.dot_general(
            gc_all[:, 128 * u : 128 * u + 128], block, NT, preferred_element_type=F32
        )
    for k in range(GZ):
        for t in range(4):
            w_out[k, 7 + t] = down[8 * k : 8 * k + 8, 128 * t : 128 * t + 128]
    sums = combine_finish(here, add_tiles, two_bufs)
    scale = lax.rsqrt(n_active)
    shift_out[...] = (sums[0:1] * scale)[:, :64]
    gain_out[...] = (sums[1:2] * scale)[:, :64]
    mean_shift, mean_gain = to_col(sums[0:1] / n_active), to_col(sums[1:2] / n_active)
    factor = gain * inverse

    def hidden_grad(v, carry):
        normed = (hid[v] - mean) * inverse
        out = mask_ref[pl.ds(v, 1), :] * factor * (g_fine[v] - (mean_shift + normed * mean_gain))
        g_cells[1 + lax.div(v, 4), 1 + lax.rem(v, 4)] = out.astype(BF16)
        return carry

    lax.fori_loop(0, 16, hidden_grad, 0)
    halo_start(here, g_cells, g_ends, g_ends_in, g_send, g_recv)
    sub_acc[...] = jnp.zeros_like(sub_acc)

    def weigh(v, carry):
        grad = g_cells[1 + lax.div(v, 4), 1 + lax.rem(v, 4)]
        sub_acc[...] += lax.dot_general(patches(stack, v), grad, NT, preferred_element_type=F32)
        return carry

    lax.fori_loop(0, 16, weigh, 0)
    sub = jnp.concatenate([sub_acc[...], jnp.zeros((32, 64), F32)], axis=0).T
    for k in range(GZ):
        for t in range(7):
            w_out[k, t] = sub[8 * k : 8 * k + 8, 128 * t : 128 * t + 128]
    for t in range(TILES, N_XY):
        p_out[t] = jnp.zeros((8, 128), F32)

    for shift in COLUMN:
        to = here.zs[shift[2]]
        send(w_out.at[to], w_in.at[here.z], w_send.at[0], w_recv.at[0], here.at(shift))
    w_in[here.z] = w_out[here.z]
    halo_finish(here, g_cells, g_ends_in, g_recv, g_edges, g_stack)

    def back(v, carry):
        out = jnp.dot(w_back[...], patches(g_stack, v), preferred_element_type=F32)
        total[pl.ds(pl.multiple_of(v * 32, 32), 32), :] = out * mask_ref[pl.ds(v, 1), :]
        return carry

    lax.fori_loop(0, 16, back, 0)
    drain(w_in.at[pl.ds(0, GZ - 1)], w_recv.at[0])
    for t in range(TILES):
        p_out[t] = add_tiles([w_in[k, t] for k in range(GZ)])
    for shift in PLANE:
        to = here.plane_at(shift)
        send(p_out.at[to], p_in.at[here.plane], w_send.at[1], w_recv.at[1], here.at(shift))
    p_in[here.plane] = p_out[here.plane]

    def spread_out(step, first):
        g = lax.rem(group + step, N_GROUP)
        tags = tag_buf[g]
        values = jnp.dot(total[...].astype(BF16), one_hot(tags), preferred_element_type=F32)
        column = tags >> 8
        out = jnp.zeros((32, CHUNK), F32)
        for v in range(16):
            out = jnp.where(column == v, values[32 * v : 32 * v + 32], out)
        out = out.astype(BF16)
        for t in range(0, GROUP, 2):
            block = out[:, 64 * t : 64 * t + 128]
            one, two = halves(block[:16], block[16:])
            home_out[g * GROUP + t] = one
            home_out[g * GROUP + t + 1] = two
        go_group(home_out, home_in, home_send, home_recv, step, first)

    def spread_step(step, carry):
        spread_out(step, 0)
        return carry

    spread_out(0, 1)
    keep_home = pltpu.make_async_copy(home_out.at[me], home_in.at[me], home_recv.at[group])
    keep_home.start()
    lax.fori_loop(1, 4, spread_step, 0)
    drain(p_in.at[pl.ds(0, N_XY - 1)], w_recv.at[1])
    f_buf[here.plane] = add_tiles([p_in[k] for k in range(N_XY)]) * scale
    for shift in PLANE:
        at = f_buf.at[here.plane]
        send(at, at, w_send.at[2], w_recv.at[2], here.at(shift))
    lax.fori_loop(4, N_GROUP, spread_step, 0)
    drain(f_buf.at[pl.ds(0, N_XY - 1)], w_recv.at[2])
    for shift in COLUMN:
        whole = f_buf.at[pl.ds(0, TILES)]
        send(whole, a_buf.at[here.z], w_send.at[3], w_recv.at[3], here.at(shift))
    for t in range(TILES):
        a_buf[here.z, t] = f_buf[t]

    def unpack(step, carry):
        g = lax.rem(group - step + N_GROUP, N_GROUP)
        drain(home_in.at[pl.ds(0, GROUP)], home_recv.at[g])
        tops, bottoms = [], []
        for t in range(0, GROUP, 2):
            top, bottom = halves(home_in[g * GROUP + t], home_in[g * GROUP + t + 1])
            tops.append(top)
            bottoms.append(bottom)
        at = pl.ds(pl.multiple_of(g * CHUNK, CHUNK), CHUNK)
        points_ref[0:16, at] = jnp.concatenate(tops, axis=1)
        points_ref[16:32, at] = jnp.concatenate(bottoms, axis=1)
        return carry

    lax.fori_loop(0, N_GROUP, unpack, 0)
    drain(a_buf.at[pl.ds(0, GZ - 1)], w_recv.at[3])
    for k in range(GZ):
        rows = slice(8 * k, 8 * k + 8)
        for t in range(6):
            sub_out[rows, 128 * t : 128 * t + 128] = a_buf[k, t]
        sub_out[rows, 768:864] = a_buf[k, 6][:, :96]
        for t in range(4):
            down_out[rows, 128 * t : 128 * t + 128] = a_buf[k, 7 + t]

    most = pl.ds(0, N_DEV - 1)
    drain(out_buf.at[most], route_send.at[0])
    drain(z_ids.at[pl.ds(0, GZ - 1)], id_send.at[0])
    drain(all_ids.at[pl.ds(0, N_XY - 1)], id_send.at[1])
    halo_drain(cells, ends_in, halo_send)
    halo_drain(g_cells, g_ends_in, g_send)
    combine_close(one_bufs)
    combine_close(two_bufs)
    drain(w_in.at[pl.ds(0, GZ - 1)], w_send.at[0])
    drain(p_in.at[pl.ds(0, N_XY - 1)], w_send.at[1])
    drain(f_buf.at[pl.ds(0, N_XY - 1)], w_send.at[2])
    drain(a_buf.at[pl.ds(0, GZ - 1)], w_send.at[3])
    drain(home_out.at[most], home_send.at[0])


def block(*operands):
    dma = pltpu.SemaphoreType.DMA
    shaped = jax.ShapeDtypeStruct
    return pl.pallas_call(
        block_kernel,
        out_shape=(
            shaped((32, 8192), BF16),
            shaped((64, 512), BF16),
            shaped((64, 864), F32),
            shaped((64, 512), F32),
            shaped((1, 64), F32),
            shaped((1, 64), F32),
        ),
        in_specs=[VMEM] * 9,
        out_specs=(VMEM,) * 6,
        scratch_shapes=[
            pltpu.VMEM((N_DEV, 16, 128), BF16),
            pltpu.VMEM((N_DEV, 16, 128), BF16),
            pltpu.VMEM((N_XY, 4, 1, 128), jnp.int32),
            pltpu.VMEM((GZ, N_XY, 1, 128), jnp.int32),
            pltpu.VMEM((N_XY, GZ, 1, 128), jnp.int32),
            pltpu.VMEM((N_GROUP, 1, CHUNK), jnp.int32),
            pltpu.VMEM((512, 256), F32),
            pltpu.VMEM((16, 256), F32),
            pltpu.VMEM((32, 27 * 64), BF16),
            pltpu.VMEM((512, 64), BF16),
            pltpu.VMEM((6, 6, 32, 256), BF16),
            pltpu.VMEM((2, 1, 512), F32),
            pltpu.VMEM((2, 9, 1, 512), F32),
            pltpu.VMEM((2, 36, 32, 128), F32),
            pltpu.VMEM((36, 96, 256), BF16),
            pltpu.VMEM((16, 64, 256), F32),
            pltpu.VMEM((4, 8, 64, 128), BF16),
            pltpu.VMEM((16, 64, 256), F32),
            pltpu.VMEM((64, 512), BF16),
            pltpu.VMEM((6, 6, 64, 256), BF16),
            pltpu.VMEM((2, 1, 1024), F32),
            pltpu.VMEM((2, 9, 1, 1024), F32),
            pltpu.VMEM((2, 36, 64, 128), F32),
            pltpu.VMEM((36, 192, 256), BF16),
            pltpu.VMEM((GZ, 8, 128), F32),
            pltpu.VMEM((N_XY, 8, 128), F32),
            pltpu.VMEM((GZ, 8, 128), F32),
            pltpu.VMEM((N_XY, 8, 128), F32),
            pltpu.VMEM((864, 64), F32),
            pltpu.VMEM((GZ, TILES, 8, 128), F32),
            pltpu.VMEM((GZ, TILES, 8, 128), F32),
            pltpu.VMEM((N_XY, 8, 128), F32),
            pltpu.VMEM((N_XY, 8, 128), F32),
            pltpu.VMEM((N_XY, 8, 128), F32),
            pltpu.VMEM((GZ, TILES, 8, 128), F32),
            pltpu.VMEM((N_DEV, 16, 128), BF16),
            pltpu.VMEM((N_DEV, 16, 128), BF16),
            dma((1,)), dma((N_GROUP,)), dma((2,)), dma((2,)), dma((2,)), dma((2,)), dma((2,)), dma((2,)),
            dma((2,)), dma((2,)), dma((2,)), dma((2,)), dma((4,)), dma((4,)), dma((1,)), dma((N_GROUP,)),
        ],
        compiler_params=pltpu.CompilerParams(collective_id=0, has_side_effects=True),
        name="block",
    )(*operands)


def on_device(
    point_feats, voxel_ids, send_counts, active, w_sub, w_down, bn_gain, bn_shift, cotangent
):
    points, coarse, grad_sub, grad_down, grad_gain, grad_shift = block(
        point_feats,
        voxel_ids.reshape(64, 128),
        send_counts,
        active,
        w_sub,
        w_down,
        bn_gain.reshape(1, 64),
        bn_shift.reshape(1, 64),
        cotangent.reshape(64, 512),
    )
    return (
        coarse.reshape(64, 2, 2, 128),
        points,
        grad_sub,
        grad_down,
        grad_gain.reshape(64),
        grad_shift.reshape(64),
    )


def solution(mesh):
    every = ("gx", "gy", "gz")
    in_specs = (
        P(None, every), P(every), P(every, None), P(*every),
        P(), P(), P(), P(), P(None, *every),
    )
    out_specs = (P(None, *every), P(None, every), P(), P(), P(), P())
    return jax.shard_map(
        on_device, mesh=mesh, in_specs=in_specs, out_specs=out_specs, check_vma=False
    )
```

time: 591 us -> 105 us (0.18); the launches traced: 583 us -> 105 us
  blocking collectives: 189 us -> 0 us
  local copies, waits for them, and re-layouts: 158 us -> 7.75 us
  other arithmetic: 99.2 us -> 0 us
  Pallas kernels: 0 us -> 96.3 us
  starting transfers between devices: 57.1 us -> 0 us
  waiting for transfers between devices: 39.4 us -> 0 us
  matrix products: 23.5 us -> 0 us
  between operations: 16.3 us -> 0.65 us
    psum x3 -> x0, blocking collectives: 189 us -> none  [the longest x1 63.5 us: on_device(): lax.psum((jnp.sum(grad_pre, axis=1), jnp.sum(grad_pre * normed, axis=1)),...]
    pallas_call x0 -> x1, Pallas kernels: none -> 96.3 us  [block(): pl.pallas_call(block_kernel, out_shape=(shaped((32, 8192), BF16), shaped(...]
    reshape x34 -> x2, local copies, waits for them, and re-layouts: 56 us -> 2.99 us  [the longest x1 1.5 us: on_device(): cotangent.reshape(64, 512)]
    scatter-add x1 -> x0, other arithmetic: 50.6 us -> none  [on_device(): jax.ops.segment_sum(arriving.T.astype(jnp.float32), target, num_segments=...]
    concatenate x18 -> x0, other arithmetic: 30.8 us -> none  [the longest x12 21.5 us: columns(): joined = jnp.concatenate(pieces, axis=0)]
    ppermute x12 -> x0, starting transfers between devices: 29.4 us -> none  [the longest x6 19.7 us: padded_2(): lax.ppermute(tail, axis, [(i, (i + 1) % count) for i in range(ends)])]
    concatenate x15 -> x0, local copies, waits for them, and re-layouts: 29 us -> none  [the longest x12 28.2 us: columns(): joined = jnp.concatenate(pieces, axis=0)]
    all_to_all x3 -> x0, starting transfers between devices: 27.3 us -> none  [the longest x1 11.5 us: on_device(): lax.all_to_all(voxel_tags, ('gx', 'gy', 'gz'), split_axis=1, concat_axis=...]
  transfers between devices with their start and end apart: 16 -> 0, of which waited for: 10 -> 0; matrix products, arithmetic and copies ran while one was open for 25% -> 0% of each run, Pallas kernels for 0% -> 0%
where the time goes in v2:
time: 105 us
  Pallas kernels  96.3 us (92%)
  local copies, waits for them, and re-layouts  7.75 us (7%)
    pallas_call x1, Pallas kernels, block(): pl.pallas_call(block_kernel, out_shape=(shaped((32, 8192), BF16), shaped(...  96.3 us
    unnamed x13, local copies, waits for them, and re-layouts  4.76 us

profile of v2, /device:TPU:1, one launch (start us, length us, event | category | flops | bytes accessed | tf_op | source)
XLA Modules:
  0.0 104.7 jit_solution(14140166745190045572)
XLA Ops:
  0.6 1.5 %reshape.36.ct_ref = bf16[64,512]{1,0:T(8,128)(2,1)} reshape(bf16[64,2,2,128]{3,2,1,0:T(2,128)(2,1)} %param.17) | data formatting | bytes 131072 | tf_op jit(solution)/shard_map/reshape | solution.py:621
  2.1 96.3 %block.1 = (bf16[32,8192]{1,0:T(8,128)(2,1)}, bf16[64,512]{1,0:T(8,128)(2,1)}, f32[64,864]{1,0:T(8,128)}, f32[64,512]{1,0:T(8,128)}, f32[1,64]{1,0:T(1,128)}, /*index=5*/f32[1,64]{1,0:T(1,128)}) custom-call(bf16[32,8192]{1,0:T(8,128)(2,1)} %feats_ref.1, s32[64,128]{1,0:T(8,128)} %bitcast.5, s32[1,128]{1,0:T(1,128)} %counts_ref.1, s32[4,4,256]{2,1,0:T(4,128)} %active_ref.1, ...), custom_call_target="tpu_custom_call" | custom-call | tf_op jit(solution)/shard_map/block/pallas_call | solution.py:551
  98.4 1.5 %reshape.37 = bf16[64,2,2,128]{3,2,1,0:T(2,128)(2,1)} reshape(bf16[64,512]{1,0:T(8,128)(2,1)} %get-tuple-element.12) | data formatting | bytes 131072 | tf_op jit(solution)/shard_map/reshape | solution.py:624
  99.9 0.0 copy-start
  99.9 1.9 %copy.20 = bf16[32,8192]{1,0:T(8,128)(2,1)} copy(bf16[32,8192]{1,0:T(8,128)(2,1)} %get-tuple-element.25) | data formatting | bytes 1048576
  101.8 0.0 copy-done
  101.8 0.0 copy-start.1
  101.8 0.7 copy.21
  102.5 0.3 copy-done.1
  102.8 0.0 copy-start.3
  102.8 0.7 copy.22
  103.5 0.0 copy-done.3
  103.5 0.0 copy-start.2
  103.5 0.5 copy.23
  104.0 0.2 copy-done.2
  104.2 0.5 copy.24
Async XLA Ops:
  99.9 1.9 %copy-start = (f32[64,864]{1,0:T(8,128)S(1)}, f32[64,864]{1,0:T(8,128)}, u32[]{:S(2)}) copy-start(f32[64,864]{1,0:T(8,128)} %get-tuple-element.26) | copy-start | bytes 663556
  101.8 1.0 copy-start.1
  102.8 0.7 copy-start.3
  103.5 0.7 copy-start.2

commit v3 on v2

--- a/solution.py
+++ b/solution.py
@@ -79,16 +79,16 @@
 
 def halo_start(here, cells, ends, ends_in, send_sem, recv_sem):
     chan = cells.shape[2]
+    for shift in SIDES:
+        a, b, _ = shift
+        src, dst = cells.at[FROM[a], FROM[b]], cells.at[INTO[a], INTO[b]]
+        send(src, dst, send_sem.at[0], recv_sem.at[0], here.at(shift))
     for k, half, edge in ((0, 0, 0), (1, 128, 127)):
         faces = jnp.concatenate(
             [cells[1 + v // 4, 1 + v % 4, :, half : half + 128] for v in range(16)], axis=0
         )
         pick = jnp.where(iota((8, 128), 1) == edge, 1.0, 0.0).astype(BF16)
         ends[k] = lax.dot_general(pick, faces, NT, preferred_element_type=F32)[0:1]
-    for shift in SIDES:
-        a, b, _ = shift
-        src, dst = cells.at[FROM[a], FROM[b]], cells.at[INTO[a], INTO[b]]
-        send(src, dst, send_sem.at[0], recv_sem.at[0], here.at(shift))
     for k, c in ((0, -1), (1, 1)):
         for a in (0, 1, -1):
             for b in (0, 1, -1):
@@ -162,8 +162,8 @@
     )
 
 
-def to_row(partial):
-    wide = jnp.concatenate([partial, jnp.zeros_like(partial)], axis=0)
+def to_row(first, second=None):
+    wide = jnp.concatenate([first, jnp.zeros_like(first) if second is None else second], axis=0)
     return jnp.sum(wide.T, axis=0, keepdims=True)
 
 
@@ -171,14 +171,6 @@
     row = row[:, :64]
     same = iota((64, 64), 0) == iota((64, 64), 1)
     return jnp.sum(jnp.where(same, row, 0.0), axis=1, keepdims=True)
-
-
-def tile_of(rows):
-    sub = iota((8, 128), 0)
-    out = jnp.zeros((8, 128), F32)
-    for k, row in enumerate(rows):
-        out = jnp.where(sub == k, row, out)
-    return out
 
 
 def combine_start(here, tile, bufs):
@@ -212,14 +204,23 @@
     return tiles[0]
 
 
+def moments(sums, squares, count):
+    return jnp.concatenate([jnp.where(iota((1, 128), 1) < 64, sums, count), squares], axis=0)
+
+
+def counts_of(tile):
+    return pltpu.roll(tile[0:1], 64, 1)
+
+
 def merge_moments(tiles):
     whole = add_tiles(tiles)
-    mean = whole[0:1] / jnp.maximum(whole[2:3], 1.0)
+    mean = whole[0:1] / jnp.maximum(counts_of(whole), 1.0)
     square = jnp.zeros((1, 128), F32)
     for t in tiles:
-        gap = t[0:1] / jnp.maximum(t[2:3], 1.0) - mean
-        square = square + (t[1:2] + t[2:3] * gap * gap)
-    return tile_of([whole[0:1], square, whole[2:3]])
+        n = counts_of(t)
+        gap = t[0:1] / jnp.maximum(n, 1.0) - mean
+        square = square + (t[1:2] + n * gap * gap)
+    return jnp.concatenate([whole[0:1], square], axis=0)
 
 
 def fold(block):
@@ -228,12 +229,12 @@
 
 def block_kernel(
     feats_ref, ids_ref, counts_ref, active_ref, w_sub_ref, w_down_ref, gain_ref, shift_ref, ct_ref,
-    points_ref, coarse_ref, sub_out, down_out, gain_out, shift_out,
-    out_buf, in_buf, out_ids, z_ids, all_ids, tag_buf, total, mask_ref, w_back, w_down_t,
+    home_in, a_buf, coarse_ref, vector_out,
+    out_buf, in_buf, out_ids, z_ids, all_ids, tag_buf, total, back_grid, mask_ref, w_band, w_back, w_down_t,
     cells, ends, ends_in, edges, stack, hid, fine, g_fine, gc_all,
     g_cells, g_ends, g_ends_in, g_edges, g_stack,
     z_one, xy_one, z_two, xy_two, sub_acc,
-    w_out, w_in, p_out, p_in, f_buf, a_buf, home_out, home_in,
+    w_out, w_in, p_out, p_in, f_buf, home_out,
     route_send, route_recv, id_send, id_recv, halo_send, halo_recv, g_send, g_recv,
     one_send, one_recv, two_send, two_recv, w_send, w_recv, home_send, home_recv,
 ):
@@ -243,13 +244,24 @@
     member = lax.rem(me, GROUP)
     barrier = pltpu.get_barrier_semaphore()
 
-    def greet(step, carry):
-        pl.semaphore_signal(
-            barrier, inc=1, device_id=lax.rem(me + step, N_DEV), device_id_type=LOGICAL
-        )
-        return carry
-
-    lax.fori_loop(1, N_DEV, greet, 0)
+    def greet(step):
+        to = lax.rem(me + step, N_DEV)
+        pl.semaphore_signal(barrier, inc=1, device_id=to, device_id_type=LOGICAL)
+
+    def greet_and_pack(m, carry):
+        greet(2 * m + 1)
+        greet(2 * m + 2)
+        block = feats_ref[:, pl.ds(pl.multiple_of(m * 128, 128), 128)]
+        first, second = halves(block[:16], block[16:])
+        out_buf[2 * m] = first
+        out_buf[2 * m + 1] = second
+        return carry
+
+    lax.fori_loop(0, 63, greet_and_pack, 0, unroll=3)
+    greet(N_DEV - 1)
+    last, final = halves(feats_ref[0:16, 8064:8192], feats_ref[16:32, 8064:8192])
+    out_buf[N_DEV - 2] = last
+    out_buf[N_DEV - 1] = final
 
     row, lane = iota((64, 128), 0), iota((64, 128), 1)
     counts = counts_ref[...]
@@ -258,16 +270,8 @@
     usable = (lane & 63) < jnp.where(lane < 64, even, odd)
     tags = jnp.where(usable, ids_ref[...], -1)
     for m in range(64):
-        out_ids[m // 4, m % 4] = tags[m : m + 1]
-
-    def pack(m, carry):
-        block = feats_ref[:, pl.ds(pl.multiple_of(m * 128, 128), 128)]
-        first, second = halves(block[:16], block[16:])
-        out_buf[2 * m] = first
-        out_buf[2 * m + 1] = second
-        return carry
-
-    lax.fori_loop(0, 64, pack, 0)
+        out_ids[m % 4, m // 4] = tags[m : m + 1]
+
     pl.semaphore_wait(barrier, N_DEV - 1)
 
     def go_group(src, dst, sends, recvs, step, first):
@@ -278,30 +282,43 @@
             send(src.at[to], dst.at[me], sends.at[0], recvs.at[group], to)
             return carry
 
-        lax.fori_loop(first, GROUP, go, 0)
+        lax.fori_loop(first, GROUP, go, 0, unroll=True)
 
     for shift in COLUMN:
         k = lax.div(here.zs[shift[2]], 2)
-        send(out_ids.at[:, k], z_ids.at[here.z], id_send.at[0], id_recv.at[0], here.at(shift))
-    z_ids[here.z] = out_ids[:, lax.div(here.z, 2)]
+        send(out_ids.at[k], z_ids.at[:, here.z], id_send.at[0], id_recv.at[0], here.at(shift))
+    z_ids[:, here.z] = out_ids[lax.div(here.z, 2)]
     keep = pltpu.make_async_copy(out_buf.at[me], in_buf.at[me], route_recv.at[group])
     keep.start()
     go_group(out_buf, in_buf, route_send, route_recv, 0, 1)
     for step in range(1, 4):
         go_group(out_buf, in_buf, route_send, route_recv, step, 0)
-    drain(z_ids.at[pl.ds(0, GZ - 1)], id_recv.at[0])
+    drain(z_ids.at[:, pl.ds(0, GZ - 1)], id_recv.at[0])
     for shift in PLANE:
         other = here.plane_at(shift)
-        send(z_ids.at[:, other], all_ids.at[here.plane], id_send.at[1], id_recv.at[1], here.at(shift))
-    all_ids[here.plane] = z_ids[:, here.plane]
+        send(z_ids.at[other], all_ids.at[here.plane], id_send.at[1], id_recv.at[1], here.at(shift))
+    all_ids[here.plane] = z_ids[here.plane]
     for step in range(4, N_GROUP):
         go_group(out_buf, in_buf, route_send, route_recv, step, 0)
 
-    turned = w_sub_ref[...].astype(F32).T.astype(BF16)
-    for e in range(0, 26, 2):
-        pair = [turned[32 * (26 - k) : 32 * (27 - k)] for k in (e, e + 1)]
-        w_back[:, 64 * e : 64 * e + 128] = jnp.concatenate(pair, axis=1)
-    w_back[:, 64 * 26 : 64 * 27] = turned[0:32]
+    weights = w_sub_ref[...].astype(F32)
+    for p in range(4):
+        parts = [jnp.zeros((64, 288 * k), F32) for k in (p, 3 - p)]
+        parts = [k for k in (parts[0], weights, parts[1]) if k.shape[1]]
+        w_band[64 * p : 64 * p + 64, :] = jnp.concatenate(parts, axis=1).astype(BF16)
+    turned = weights.T
+    gap = jnp.zeros((32, 192), F32)
+    for a in range(3):
+        taps = [turned[32 * (26 - e) : 32 * (27 - e)] for e in range(9 * a, 9 * a + 9)]
+        for b in range(2):
+            row = jnp.concatenate([gap] * b + taps + [gap] * (1 - b), axis=1).astype(BF16)
+            for p in range(4):
+                at = 32 * (2 * p + b)
+                w_back[at : at + 32, 768 * (p + a) : 768 * (p + a + 1)] = row
+    for p in range(4):
+        for x in range(6):
+            if not 0 <= x - p <= 2:
+                w_back[64 * p : 64 * p + 64, 768 * x : 768 * x + 768] = jnp.zeros((64, 768), BF16)
     w_down_t[...] = w_down_ref[...].astype(F32).T.astype(BF16)
     z = iota((256, 256), 0)
     order = jnp.where((z >> 1) + (z & 1) * 128 == iota((256, 256), 1), 1.0, 0.0)
@@ -311,6 +328,7 @@
     count = jnp.sum(jnp.sum(mask, axis=0, keepdims=True), axis=1, keepdims=True)
 
     coarse_masks = []
+    cotangent = ct_ref[...].astype(F32)
     for u in range(4):
         up, uq = u // 2, u % 2
         seen = jnp.zeros((1, 128), F32)
@@ -319,7 +337,7 @@
                 v = (2 * up + a) * 4 + 2 * uq + b
                 seen = jnp.maximum(seen, jnp.maximum(mask[v : v + 1, 0:128], mask[v : v + 1, 128:256]))
         coarse_masks.append(seen)
-        grad_c = (ct_ref[:, 128 * u : 128 * u + 128].astype(F32) * seen).astype(BF16)
+        grad_c = (cotangent[:, up, uq] * seen).astype(BF16)
         gc_all[:, 128 * u : 128 * u + 128] = grad_c
         pulled = jnp.dot(w_down_t[...], grad_c, preferred_element_type=F32)
         for a in range(2):
@@ -366,13 +384,17 @@
     one_bufs = (z_one, xy_one, one_send, one_recv)
     two_bufs = (z_two, xy_two, two_send, two_recv)
 
-    def conv(v, acc):
-        out = jnp.dot(w_sub_ref[...], patches(stack, v), preferred_element_type=F32)
-        out = out * mask_ref[pl.ds(v, 1), :]
-        hid[v] = out
-        return acc + fold(out)
-
-    summed = lax.fori_loop(0, 16, conv, jnp.zeros((64, 128), F32))
+    def conv(q, acc):
+        slab = jnp.concatenate([stack[pl.ds(6 * x + q, 3)].reshape(288, 256) for x in range(6)], axis=0)
+        out = jnp.dot(w_band[...], slab, preferred_element_type=F32)
+        for p in range(4):
+            v = 4 * p + q
+            part = out[64 * p : 64 * p + 64] * mask_ref[pl.ds(v, 1), :]
+            hid[v] = part
+            acc = acc + fold(part)
+        return acc
+
+    summed = lax.fori_loop(0, 4, conv, jnp.zeros((64, 128), F32))
     own_mean = jnp.sum(summed, axis=1, keepdims=True) / jnp.maximum(count, 1.0)
 
     def spread(v, acc):
@@ -380,11 +402,10 @@
         return acc + fold(gap * gap)
 
     square = lax.fori_loop(0, 16, spread, jnp.zeros((64, 128), F32))
-    count_row = jnp.broadcast_to(count, (1, 128))
-    combine_start(here, tile_of([to_row(summed), to_row(square), count_row]), one_bufs)
+    combine_start(here, moments(to_row(summed), to_row(square), count), one_bufs)
     gain, shift = to_col(gain_ref[...]), to_col(shift_ref[...])
     merged = combine_finish(here, merge_moments, one_bufs)
-    n_active = merged[2:3]
+    n_active = jnp.where(iota((1, 128), 1) < 64, counts_of(merged), merged[0:1])
     mean = to_col(merged[0:1] / n_active)
     inverse = to_col(lax.rsqrt(merged[1:2] / n_active + EPS))
 
@@ -408,7 +429,7 @@
 
     zero = jnp.zeros((64, 128), F32)
     sum_shift, sum_gain = lax.fori_loop(0, 16, norm, (zero, zero))
-    combine_start(here, tile_of([to_row(sum_shift), to_row(sum_gain)]), two_bufs)
+    combine_start(here, to_row(sum_shift, sum_gain), two_bufs)
     down = jnp.zeros((64, 512), F32)
     for u in range(4):
         block = fine[u].reshape(512, 128)
@@ -422,9 +443,9 @@
             w_out[k, 7 + t] = down[8 * k : 8 * k + 8, 128 * t : 128 * t + 128]
     sums = combine_finish(here, add_tiles, two_bufs)
     scale = lax.rsqrt(n_active)
-    shift_out[...] = (sums[0:1] * scale)[:, :64]
-    gain_out[...] = (sums[1:2] * scale)[:, :64]
-    mean_shift, mean_gain = to_col(sums[0:1] / n_active), to_col(sums[1:2] / n_active)
+    vector_out[...] = sums * scale
+    averages = sums / n_active
+    mean_shift, mean_gain = to_col(averages), to_col(pltpu.roll(averages, 64, 1))
     factor = gain * inverse
 
     def hidden_grad(v, carry):
@@ -456,12 +477,20 @@
     w_in[here.z] = w_out[here.z]
     halo_finish(here, g_cells, g_ends_in, g_recv, g_edges, g_stack)
 
-    def back(v, carry):
-        out = jnp.dot(w_back[...], patches(g_stack, v), preferred_element_type=F32)
-        total[pl.ds(pl.multiple_of(v * 32, 32), 32), :] = out * mask_ref[pl.ds(v, 1), :]
-        return carry
-
-    lax.fori_loop(0, 16, back, 0)
+    def back(h, carry):
+        slab = jnp.concatenate(
+            [g_stack[pl.ds(6 * x + 2 * h, 4)].reshape(768, 256) for x in range(6)], axis=0
+        )
+        out = jnp.dot(w_back[...], slab, preferred_element_type=F32)
+        for p in range(4):
+            for b in range(2):
+                v = 4 * p + 2 * h + b
+                at = 32 * (2 * p + b)
+                part = out[at : at + 32] * mask_ref[pl.ds(v, 1), :]
+                back_grid[pl.ds(pl.multiple_of(v * 32, 32), 32), :] = part.astype(BF16)
+        return carry
+
+    lax.fori_loop(0, 2, back, 0)
     drain(w_in.at[pl.ds(0, GZ - 1)], w_recv.at[0])
     for t in range(TILES):
         p_out[t] = add_tiles([w_in[k, t] for k in range(GZ)])
@@ -473,7 +502,7 @@
     def spread_out(step, first):
         g = lax.rem(group + step, N_GROUP)
         tags = tag_buf[g]
-        values = jnp.dot(total[...].astype(BF16), one_hot(tags), preferred_element_type=F32)
+        values = jnp.dot(back_grid[...], one_hot(tags), preferred_element_type=F32)
         column = tags >> 8
         out = jnp.zeros((32, CHUNK), F32)
         for v in range(16):
@@ -507,32 +536,12 @@
     for t in range(TILES):
         a_buf[here.z, t] = f_buf[t]
 
-    def unpack(step, carry):
-        g = lax.rem(group - step + N_GROUP, N_GROUP)
+    for g in range(N_GROUP):
         drain(home_in.at[pl.ds(0, GROUP)], home_recv.at[g])
-        tops, bottoms = [], []
-        for t in range(0, GROUP, 2):
-            top, bottom = halves(home_in[g * GROUP + t], home_in[g * GROUP + t + 1])
-            tops.append(top)
-            bottoms.append(bottom)
-        at = pl.ds(pl.multiple_of(g * CHUNK, CHUNK), CHUNK)
-        points_ref[0:16, at] = jnp.concatenate(tops, axis=1)
-        points_ref[16:32, at] = jnp.concatenate(bottoms, axis=1)
-        return carry
-
-    lax.fori_loop(0, N_GROUP, unpack, 0)
     drain(a_buf.at[pl.ds(0, GZ - 1)], w_recv.at[3])
-    for k in range(GZ):
-        rows = slice(8 * k, 8 * k + 8)
-        for t in range(6):
-            sub_out[rows, 128 * t : 128 * t + 128] = a_buf[k, t]
-        sub_out[rows, 768:864] = a_buf[k, 6][:, :96]
-        for t in range(4):
-            down_out[rows, 128 * t : 128 * t + 128] = a_buf[k, 7 + t]
-
     most = pl.ds(0, N_DEV - 1)
     drain(out_buf.at[most], route_send.at[0])
-    drain(z_ids.at[pl.ds(0, GZ - 1)], id_send.at[0])
+    drain(z_ids.at[:, pl.ds(0, GZ - 1)], id_send.at[0])
     drain(all_ids.at[pl.ds(0, N_XY - 1)], id_send.at[1])
     halo_drain(cells, ends_in, halo_send)
     halo_drain(g_cells, g_ends_in, g_send)
@@ -551,25 +560,25 @@
     return pl.pallas_call(
         block_kernel,
         out_shape=(
-            shaped((32, 8192), BF16),
+            shaped((N_DEV, 16, 128), BF16),
+            shaped((GZ, TILES, 8, 128), F32),
             shaped((64, 512), BF16),
-            shaped((64, 864), F32),
-            shaped((64, 512), F32),
-            shaped((1, 64), F32),
-            shaped((1, 64), F32),
+            shaped((1, 128), F32),
         ),
         in_specs=[VMEM] * 9,
-        out_specs=(VMEM,) * 6,
+        out_specs=(VMEM,) * 4,
         scratch_shapes=[
             pltpu.VMEM((N_DEV, 16, 128), BF16),
             pltpu.VMEM((N_DEV, 16, 128), BF16),
-            pltpu.VMEM((N_XY, 4, 1, 128), jnp.int32),
-            pltpu.VMEM((GZ, N_XY, 1, 128), jnp.int32),
+            pltpu.VMEM((4, N_XY, 1, 128), jnp.int32),
+            pltpu.VMEM((N_XY, GZ, 1, 128), jnp.int32),
             pltpu.VMEM((N_XY, GZ, 1, 128), jnp.int32),
             pltpu.VMEM((N_GROUP, 1, CHUNK), jnp.int32),
             pltpu.VMEM((512, 256), F32),
+            pltpu.VMEM((512, 256), BF16),
             pltpu.VMEM((16, 256), F32),
-            pltpu.VMEM((32, 27 * 64), BF16),
+            pltpu.VMEM((256, 6 * 288), BF16),
+            pltpu.VMEM((256, 6 * 768), BF16),
             pltpu.VMEM((512, 64), BF16),
             pltpu.VMEM((6, 6, 32, 256), BF16),
             pltpu.VMEM((2, 1, 512), F32),
@@ -585,18 +594,16 @@
             pltpu.VMEM((2, 9, 1, 1024), F32),
             pltpu.VMEM((2, 36, 64, 128), F32),
             pltpu.VMEM((36, 192, 256), BF16),
-            pltpu.VMEM((GZ, 8, 128), F32),
-            pltpu.VMEM((N_XY, 8, 128), F32),
-            pltpu.VMEM((GZ, 8, 128), F32),
-            pltpu.VMEM((N_XY, 8, 128), F32),
+            pltpu.VMEM((GZ, 2, 128), F32),
+            pltpu.VMEM((N_XY, 2, 128), F32),
+            pltpu.VMEM((GZ, 1, 128), F32),
+            pltpu.VMEM((N_XY, 1, 128), F32),
             pltpu.VMEM((864, 64), F32),
             pltpu.VMEM((GZ, TILES, 8, 128), F32),
             pltpu.VMEM((GZ, TILES, 8, 128), F32),
             pltpu.VMEM((N_XY, 8, 128), F32),
             pltpu.VMEM((N_XY, 8, 128), F32),
             pltpu.VMEM((N_XY, 8, 128), F32),
-            pltpu.VMEM((GZ, TILES, 8, 128), F32),
-            pltpu.VMEM((N_DEV, 16, 128), BF16),
             pltpu.VMEM((N_DEV, 16, 128), BF16),
             dma((1,)), dma((N_GROUP,)), dma((2,)), dma((2,)), dma((2,)), dma((2,)), dma((2,)), dma((2,)),
             dma((2,)), dma((2,)), dma((2,)), dma((2,)), dma((4,)), dma((4,)), dma((1,)), dma((N_GROUP,)),
@@ -606,10 +613,33 @@
     )(*operands)
 
 
+def finish_kernel(home_ref, sums_ref, coarse_ref, vector_ref, points_ref, fine_ref, sub_ref, down_ref, gain_ref, shift_ref):
+    def unpack(m, carry):
+        top, bottom = halves(home_ref[2 * m], home_ref[2 * m + 1])
+        at = pl.ds(pl.multiple_of(m * 128, 128), 128)
+        points_ref[0:16, at] = top
+        points_ref[16:32, at] = bottom
+        return carry
+
+    lax.fori_loop(0, 64, unpack, 0, unroll=8)
+    for k in range(GZ):
+        rows = slice(8 * k, 8 * k + 8)
+        for t in range(6):
+            sub_ref[rows, 128 * t : 128 * t + 128] = sums_ref[k, t]
+        sub_ref[rows, 768:864] = sums_ref[k, 6][:, :96]
+        for t in range(4):
+            down_ref[rows, 128 * t : 128 * t + 128] = sums_ref[k, 7 + t]
+    coarse = coarse_ref[...].astype(F32)
+    parts = [coarse[:, 128 * u : 128 * u + 128].reshape(64, 1, 128) for u in range(4)]
+    fine_ref[...] = jnp.concatenate(parts, axis=1).reshape(64, 2, 2, 128).astype(BF16)
+    shift_ref[...] = vector_ref[:, :64]
+    gain_ref[...] = vector_ref[:, 64:]
+
+
 def on_device(
     point_feats, voxel_ids, send_counts, active, w_sub, w_down, bn_gain, bn_shift, cotangent
 ):
-    points, coarse, grad_sub, grad_down, grad_gain, grad_shift = block(
+    parts = block(
         point_feats,
         voxel_ids.reshape(64, 128),
         send_counts,
@@ -618,16 +648,24 @@
         w_down,
         bn_gain.reshape(1, 64),
         bn_shift.reshape(1, 64),
-        cotangent.reshape(64, 512),
+        cotangent,
     )
-    return (
-        coarse.reshape(64, 2, 2, 128),
-        points,
-        grad_sub,
-        grad_down,
-        grad_gain.reshape(64),
-        grad_shift.reshape(64),
-    )
+    shaped = jax.ShapeDtypeStruct
+    points, coarse, grad_sub, grad_down, grad_gain, grad_shift = pl.pallas_call(
+        finish_kernel,
+        out_shape=(
+            shaped((32, 8192), BF16),
+            shaped((64, 2, 2, 128), BF16),
+            shaped((64, 864), F32),
+            shaped((64, 512), F32),
+            shaped((1, 64), F32),
+            shaped((1, 64), F32),
+        ),
+        in_specs=[VMEM] * 4,
+        out_specs=(VMEM,) * 6,
+        name="finish",
+    )(*parts)
+    return coarse, points, grad_sub, grad_down, grad_gain.reshape(64), grad_shift.reshape(64)
 
 
 def solution(mesh):

time: 105 us -> 94.5 us (0.900)
  local copies, waits for them, and re-layouts: 7.75 us -> 0 us
  Pallas kernels: 96.3 us -> 93.7 us
    unnamed x13 -> x0, local copies, waits for them, and re-layouts: 4.76 us -> none
    reshape x2 -> x0, local copies, waits for them, and re-layouts: 2.99 us -> none  [the longest x1 1.5 us: on_device(): cotangent.reshape(64, 512)]
    pallas_call x1 -> x2, Pallas kernels: 96.3 us -> 93.7 us  [the longest x1 90.9 us: block(): pl.pallas_call(block_kernel, out_shape=(shaped((N_DEV, 16, 128), BF16), s...]
where the time goes in v3:
time: 94.5 us; the launch traced here: 94.3 us
  Pallas kernels  93.7 us (99%)
    pallas_call x1, Pallas kernels, block(): pl.pallas_call(block_kernel, out_shape=(shaped((N_DEV, 16, 128), BF16), s...  90.9 us
    pallas_call x1, Pallas kernels, on_device(): pl.pallas_call(finish_kernel, out_shape=(shaped((32, 8192), BF16), shaped...  2.8 us

profile of v3, /device:TPU:1, one launch (start us, length us, event | category | flops | bytes accessed | tf_op | source)
XLA Modules:
  0.0 94.3 jit_solution(14848362434167257892)
XLA Ops:
  0.6 90.9 %block.1 = (bf16[128,16,128]{2,1,0:T(8,128)(2,1)}, f32[8,11,8,128]{3,2,1,0:T(8,128)}, bf16[64,512]{1,0:T(8,128)(2,1)}, f32[1,128]{1,0:T(1,128)}) custom-call(bf16[32,8192]{1,0:T(8,128)(2,1)} %feats_ref.1, s32[64,128]{1,0:T(8,128)} %bitcast.5, s32[1,128]{1,0:T(1,128)} %counts_ref.1, s32[4,4,256]{2,1,0:T(4,128)} %active_ref.1, bf16[64,864]{1,0:T(8,128)(2,1)} %w_sub_ref.1, ...), custom_call_target="tpu_custom_call" | custom-call | tf_op jit(solution)/shard_map/block/pallas_call | solution.py:560
  91.5 2.8 %finish.1 = (bf16[32,8192]{1,0:T(8,128)(2,1)}, bf16[64,2,2,128]{3,2,1,0:T(2,128)(2,1)}, f32[64,864]{1,0:T(8,128)}, f32[64,512]{1,0:T(8,128)}, f32[1,64]{1,0:T(1,128)}, /*index=5*/f32[1,64]{1,0:T(1,128)}) custom-call(bf16[128,16,128]{2,1,0:T(8,128)(2,1)} %get-tuple-element.16.home_ref, f32[8,11,8,128]{3,2,1,0:T(8,128)} %get-tuple-element.17.sums_ref, ...), custom_call_target="tpu_custom_call" | custom-call | tf_op jit(solution)/shard_map/finish/pallas_call | solution.py:654

commit v4 on v3

--- a/solution.py
+++ b/solution.py
@@ -151,7 +151,7 @@
         stack[v, 2 * chan : 3 * chan, 128:256] = nxt.astype(BF16)
         return carry
 
-    lax.fori_loop(0, 36, body, 0)
+    lax.fori_loop(0, 36, body, 0, unroll=4)
 
 
 def patches(stack, v):
@@ -230,7 +230,7 @@
 def block_kernel(
     feats_ref, ids_ref, counts_ref, active_ref, w_sub_ref, w_down_ref, gain_ref, shift_ref, ct_ref,
     home_in, a_buf, coarse_ref, vector_out,
-    out_buf, in_buf, out_ids, z_ids, all_ids, tag_buf, total, back_grid, mask_ref, w_band, w_back, w_down_t,
+    out_buf, in_buf, out_ids, z_ids, all_ids, tag_buf, pick_buf, total, back_grid, mask_ref, w_band, w_back, w_down_t,
     cells, ends, ends_in, edges, stack, hid, fine, g_fine, gc_all,
     g_cells, g_ends, g_ends_in, g_edges, g_stack,
     z_one, xy_one, z_two, xy_two, sub_acc,
@@ -244,24 +244,13 @@
     member = lax.rem(me, GROUP)
     barrier = pltpu.get_barrier_semaphore()
 
-    def greet(step):
-        to = lax.rem(me + step, N_DEV)
-        pl.semaphore_signal(barrier, inc=1, device_id=to, device_id_type=LOGICAL)
-
-    def greet_and_pack(m, carry):
-        greet(2 * m + 1)
-        greet(2 * m + 2)
-        block = feats_ref[:, pl.ds(pl.multiple_of(m * 128, 128), 128)]
-        first, second = halves(block[:16], block[16:])
-        out_buf[2 * m] = first
-        out_buf[2 * m + 1] = second
-        return carry
-
-    lax.fori_loop(0, 63, greet_and_pack, 0, unroll=3)
-    greet(N_DEV - 1)
-    last, final = halves(feats_ref[0:16, 8064:8192], feats_ref[16:32, 8064:8192])
-    out_buf[N_DEV - 2] = last
-    out_buf[N_DEV - 1] = final
+    def greet(step, carry):
+        pl.semaphore_signal(
+            barrier, inc=1, device_id=lax.rem(me + step, N_DEV), device_id_type=LOGICAL
+        )
+        return carry
+
+    lax.fori_loop(1, N_DEV, greet, 0, unroll=True)
 
     row, lane = iota((64, 128), 0), iota((64, 128), 1)
     counts = counts_ref[...]
@@ -288,64 +277,39 @@
         k = lax.div(here.zs[shift[2]], 2)
         send(out_ids.at[k], z_ids.at[:, here.z], id_send.at[0], id_recv.at[0], here.at(shift))
     z_ids[:, here.z] = out_ids[lax.div(here.z, 2)]
+
+    def pack_group(step):
+        g = lax.rem(group + step, N_GROUP)
+        points = feats_ref[:, pl.ds(pl.multiple_of(g * CHUNK, CHUNK), CHUNK)]
+        for t in range(0, GROUP, 2):
+            block = points[:, 64 * t : 64 * t + 128]
+            first, second = halves(block[:16], block[16:])
+            out_buf[g * GROUP + t] = first
+            out_buf[g * GROUP + t + 1] = second
+
+    def route_step(step, carry):
+        pack_group(step)
+        go_group(out_buf, in_buf, route_send, route_recv, step, 0)
+        return carry
+
+    pack_group(0)
     keep = pltpu.make_async_copy(out_buf.at[me], in_buf.at[me], route_recv.at[group])
     keep.start()
     go_group(out_buf, in_buf, route_send, route_recv, 0, 1)
-    for step in range(1, 4):
-        go_group(out_buf, in_buf, route_send, route_recv, step, 0)
+    lax.fori_loop(1, 4, route_step, 0)
     drain(z_ids.at[:, pl.ds(0, GZ - 1)], id_recv.at[0])
     for shift in PLANE:
         other = here.plane_at(shift)
         send(z_ids.at[other], all_ids.at[here.plane], id_send.at[1], id_recv.at[1], here.at(shift))
     all_ids[here.plane] = z_ids[here.plane]
-    for step in range(4, N_GROUP):
-        go_group(out_buf, in_buf, route_send, route_recv, step, 0)
-
-    weights = w_sub_ref[...].astype(F32)
-    for p in range(4):
-        parts = [jnp.zeros((64, 288 * k), F32) for k in (p, 3 - p)]
-        parts = [k for k in (parts[0], weights, parts[1]) if k.shape[1]]
-        w_band[64 * p : 64 * p + 64, :] = jnp.concatenate(parts, axis=1).astype(BF16)
-    turned = weights.T
-    gap = jnp.zeros((32, 192), F32)
-    for a in range(3):
-        taps = [turned[32 * (26 - e) : 32 * (27 - e)] for e in range(9 * a, 9 * a + 9)]
-        for b in range(2):
-            row = jnp.concatenate([gap] * b + taps + [gap] * (1 - b), axis=1).astype(BF16)
-            for p in range(4):
-                at = 32 * (2 * p + b)
-                w_back[at : at + 32, 768 * (p + a) : 768 * (p + a + 1)] = row
-    for p in range(4):
-        for x in range(6):
-            if not 0 <= x - p <= 2:
-                w_back[64 * p : 64 * p + 64, 768 * x : 768 * x + 768] = jnp.zeros((64, 768), BF16)
-    w_down_t[...] = w_down_ref[...].astype(F32).T.astype(BF16)
+    lax.fori_loop(4, N_GROUP, route_step, 0)
+
     z = iota((256, 256), 0)
     order = jnp.where((z >> 1) + (z & 1) * 128 == iota((256, 256), 1), 1.0, 0.0)
     active = jnp.concatenate([active_ref[p] for p in range(4)], axis=0).astype(F32)
     mask = jnp.dot(active.astype(BF16), order.astype(BF16), preferred_element_type=F32)
     mask_ref[...] = mask
     count = jnp.sum(jnp.sum(mask, axis=0, keepdims=True), axis=1, keepdims=True)
-
-    coarse_masks = []
-    cotangent = ct_ref[...].astype(F32)
-    for u in range(4):
-        up, uq = u // 2, u % 2
-        seen = jnp.zeros((1, 128), F32)
-        for a in range(2):
-            for b in range(2):
-                v = (2 * up + a) * 4 + 2 * uq + b
-                seen = jnp.maximum(seen, jnp.maximum(mask[v : v + 1, 0:128], mask[v : v + 1, 128:256]))
-        coarse_masks.append(seen)
-        grad_c = (cotangent[:, up, uq] * seen).astype(BF16)
-        gc_all[:, 128 * u : 128 * u + 128] = grad_c
-        pulled = jnp.dot(w_down_t[...], grad_c, preferred_element_type=F32)
-        for a in range(2):
-            for b in range(2):
-                for c in range(2):
-                    at = ((a * 2 + b) * 2 + c) * 64
-                    v = (2 * up + a) * 4 + 2 * uq + b
-                    g_fine[v, :, 128 * c : 128 * c + 128] = pulled[at : at + 64]
 
     total[...] = jnp.zeros_like(total)
     low = iota((1, 128), 1) < 64
@@ -373,13 +337,56 @@
         spread = jnp.concatenate(
             [jnp.where(column == v, x, 0.0).astype(BF16) for v in range(16)], axis=0
         )
-        total[...] += lax.dot_general(spread, one_hot(tags), NT, preferred_element_type=F32)
+        picks = one_hot(tags)
+        pick_buf[g] = picks
+        total[...] += lax.dot_general(spread, picks, NT, preferred_element_type=F32)
         return carry
 
     lax.fori_loop(0, N_GROUP, collect, 0)
     for v in range(16):
         cells[1 + v // 4, 1 + v % 4] = (total[32 * v : 32 * v + 32, :] * mask[v : v + 1]).astype(BF16)
     halo_start(here, cells, ends, ends_in, halo_send, halo_recv)
+
+    weights = w_sub_ref[...].astype(F32)
+    for p in range(4):
+        parts = [jnp.zeros((64, 288 * k), F32) for k in (p, 3 - p)]
+        parts = [k for k in (parts[0], weights, parts[1]) if k.shape[1]]
+        w_band[64 * p : 64 * p + 64, :] = jnp.concatenate(parts, axis=1).astype(BF16)
+    turned = weights.T
+    gap = jnp.zeros((32, 192), F32)
+    for a in range(3):
+        taps = [turned[32 * (26 - e) : 32 * (27 - e)] for e in range(9 * a, 9 * a + 9)]
+        for b in range(2):
+            row = jnp.concatenate([gap] * b + taps + [gap] * (1 - b), axis=1).astype(BF16)
+            for p in range(4):
+                at = 32 * (2 * p + b)
+                w_back[at : at + 32, 768 * (p + a) : 768 * (p + a + 1)] = row
+    for p in range(4):
+        for x in range(6):
+            if not 0 <= x - p <= 2:
+                w_back[64 * p : 64 * p + 64, 768 * x : 768 * x + 768] = jnp.zeros((64, 768), BF16)
+    w_down_t[...] = w_down_ref[...].astype(F32).T.astype(BF16)
+
+    coarse_masks = []
+    cotangent = ct_ref[...].astype(F32)
+    for u in range(4):
+        up, uq = u // 2, u % 2
+        seen = jnp.zeros((1, 128), F32)
+        for a in range(2):
+            for b in range(2):
+                v = (2 * up + a) * 4 + 2 * uq + b
+                seen = jnp.maximum(seen, jnp.maximum(mask[v : v + 1, 0:128], mask[v : v + 1, 128:256]))
+        coarse_masks.append(seen)
+        grad_c = (cotangent[:, up, uq] * seen).astype(BF16)
+        gc_all[:, 128 * u : 128 * u + 128] = grad_c
+        pulled = jnp.dot(w_down_t[...], grad_c, preferred_element_type=F32)
+        for a in range(2):
+            for b in range(2):
+                for c in range(2):
+                    at = ((a * 2 + b) * 2 + c) * 64
+                    v = (2 * up + a) * 4 + 2 * uq + b
+                    g_fine[v, :, 128 * c : 128 * c + 128] = pulled[at : at + 64]
+
     halo_finish(here, cells, ends_in, halo_recv, edges, stack)
     one_bufs = (z_one, xy_one, one_send, one_recv)
     two_bufs = (z_two, xy_two, two_send, two_recv)
@@ -499,11 +506,10 @@
         send(p_out.at[to], p_in.at[here.plane], w_send.at[1], w_recv.at[1], here.at(shift))
     p_in[here.plane] = p_out[here.plane]
 
-    def spread_out(step, first):
+    def spread_out(step):
         g = lax.rem(group + step, N_GROUP)
-        tags = tag_buf[g]
-        values = jnp.dot(back_grid[...], one_hot(tags), preferred_element_type=F32)
-        column = tags >> 8
+        column = tag_buf[g] >> 8
+        values = jnp.dot(back_grid[...], pick_buf[g], preferred_element_type=F32)
         out = jnp.zeros((32, CHUNK), F32)
         for v in range(16):
             out = jnp.where(column == v, values[32 * v : 32 * v + 32], out)
@@ -513,28 +519,31 @@
             one, two = halves(block[:16], block[16:])
             home_out[g * GROUP + t] = one
             home_out[g * GROUP + t + 1] = two
-        go_group(home_out, home_in, home_send, home_recv, step, first)
 
     def spread_step(step, carry):
-        spread_out(step, 0)
-        return carry
-
-    spread_out(0, 1)
+        go_group(home_out, home_in, home_send, home_recv, step - 1, 0)
+        spread_out(step)
+        return carry
+
+    spread_out(0)
     keep_home = pltpu.make_async_copy(home_out.at[me], home_in.at[me], home_recv.at[group])
     keep_home.start()
-    lax.fori_loop(1, 4, spread_step, 0)
+    go_group(home_out, home_in, home_send, home_recv, 0, 1)
+    spread_out(1)
     drain(p_in.at[pl.ds(0, N_XY - 1)], w_recv.at[1])
     f_buf[here.plane] = add_tiles([p_in[k] for k in range(N_XY)]) * scale
     for shift in PLANE:
         at = f_buf.at[here.plane]
         send(at, at, w_send.at[2], w_recv.at[2], here.at(shift))
-    lax.fori_loop(4, N_GROUP, spread_step, 0)
+    lax.fori_loop(2, 4, spread_step, 0)
     drain(f_buf.at[pl.ds(0, N_XY - 1)], w_recv.at[2])
     for shift in COLUMN:
         whole = f_buf.at[pl.ds(0, TILES)]
         send(whole, a_buf.at[here.z], w_send.at[3], w_recv.at[3], here.at(shift))
     for t in range(TILES):
         a_buf[here.z, t] = f_buf[t]
+    lax.fori_loop(4, N_GROUP, spread_step, 0)
+    go_group(home_out, home_in, home_send, home_recv, N_GROUP - 1, 0)
 
     for g in range(N_GROUP):
         drain(home_in.at[pl.ds(0, GROUP)], home_recv.at[g])
@@ -574,6 +583,7 @@
             pltpu.VMEM((N_XY, GZ, 1, 128), jnp.int32),
             pltpu.VMEM((N_XY, GZ, 1, 128), jnp.int32),
             pltpu.VMEM((N_GROUP, 1, CHUNK), jnp.int32),
+            pltpu.VMEM((N_GROUP, 256, CHUNK), BF16),
             pltpu.VMEM((512, 256), F32),
             pltpu.VMEM((512, 256), BF16),
             pltpu.VMEM((16, 256), F32),

time: 94.5 us -> 89.1 us (0.943)
  Pallas kernels: 93.7 us -> 88.4 us
    pallas_call x1, Pallas kernels: 90.9 us -> 85.5 us  [block(): pl.pallas_call(block_kernel, out_shape=(shaped((N_DEV, 16, 128), BF16), s...]
where the time goes in v4:
time: 89.1 us; the launch traced here: 89 us
  Pallas kernels  88.4 us (99%)
    pallas_call x1, Pallas kernels, block(): pl.pallas_call(block_kernel, out_shape=(shaped((N_DEV, 16, 128), BF16), s...  85.5 us
    pallas_call x1, Pallas kernels, on_device(): pl.pallas_call(finish_kernel, out_shape=(shaped((32, 8192), BF16), shaped...  2.8 us

profile of v4, /device:TPU:1, one launch (start us, length us, event | category | flops | bytes accessed | tf_op | source)
XLA Modules:
  0.0 89.0 jit_solution(13950504959453711070)
XLA Ops:
  0.6 85.5 %block.1 = (bf16[128,16,128]{2,1,0:T(8,128)(2,1)}, f32[8,11,8,128]{3,2,1,0:T(8,128)}, bf16[64,512]{1,0:T(8,128)(2,1)}, f32[1,128]{1,0:T(1,128)}) custom-call(bf16[32,8192]{1,0:T(8,128)(2,1)} %feats_ref.1, s32[64,128]{1,0:T(8,128)} %bitcast.5, s32[1,128]{1,0:T(1,128)} %counts_ref.1, s32[4,4,256]{2,1,0:T(4,128)} %active_ref.1, bf16[64,864]{1,0:T(8,128)(2,1)} %w_sub_ref.1, ...), custom_call_target="tpu_custom_call" | custom-call | tf_op jit(solution)/shard_map/block/pallas_call | solution.py:569
  86.2 2.8 %finish.1 = (bf16[32,8192]{1,0:T(8,128)(2,1)}, bf16[64,2,2,128]{3,2,1,0:T(2,128)(2,1)}, f32[64,864]{1,0:T(8,128)}, f32[64,512]{1,0:T(8,128)}, f32[1,64]{1,0:T(1,128)}, /*index=5*/f32[1,64]{1,0:T(1,128)}) custom-call(bf16[128,16,128]{2,1,0:T(8,128)(2,1)} %get-tuple-element.16.home_ref, f32[8,11,8,128]{3,2,1,0:T(8,128)} %get-tuple-element.17.sums_ref, ...), custom_call_target="tpu_custom_call" | custom-call | tf_op jit(solution)/shard_map/finish/pallas_call | solution.py:664

commit v5 on v4

--- a/solution.py
+++ b/solution.py
@@ -230,7 +230,7 @@
 def block_kernel(
     feats_ref, ids_ref, counts_ref, active_ref, w_sub_ref, w_down_ref, gain_ref, shift_ref, ct_ref,
     home_in, a_buf, coarse_ref, vector_out,
-    out_buf, in_buf, out_ids, z_ids, all_ids, tag_buf, pick_buf, total, back_grid, mask_ref, w_band, w_back, w_down_t,
+    out_buf, in_buf, out_ids, z_ids, plane_ids, all_ids, tag_buf, pick_buf, total, back_grid, mask_ref, w_band, w_back, w_down_t,
     cells, ends, ends_in, edges, stack, hid, fine, g_fine, gc_all,
     g_cells, g_ends, g_ends_in, g_edges, g_stack,
     z_one, xy_one, z_two, xy_two, sub_acc,
@@ -258,8 +258,12 @@
     odd = jnp.sum(jnp.where(lane == 2 * row + 1, counts, 0), axis=1, keepdims=True)
     usable = (lane & 63) < jnp.where(lane < 64, even, odd)
     tags = jnp.where(usable, ids_ref[...], -1)
-    for m in range(64):
-        out_ids[m % 4, m // 4] = tags[m : m + 1]
+    for k in range(4):
+        for pair in range(8):
+            m = 8 * pair + k
+            first, second = halves(tags[m : m + 1], tags[m + 4 : m + 5])
+            out_ids[2 * k, pair] = first
+            out_ids[2 * k + 1, pair] = second
 
     pl.semaphore_wait(barrier, N_DEV - 1)
 
@@ -274,9 +278,9 @@
         lax.fori_loop(first, GROUP, go, 0, unroll=True)
 
     for shift in COLUMN:
-        k = lax.div(here.zs[shift[2]], 2)
-        send(out_ids.at[k], z_ids.at[:, here.z], id_send.at[0], id_recv.at[0], here.at(shift))
-    z_ids[:, here.z] = out_ids[lax.div(here.z, 2)]
+        k = here.zs[shift[2]]
+        send(out_ids.at[k], z_ids.at[here.z], id_send.at[0], id_recv.at[0], here.at(shift))
+    z_ids[here.z] = out_ids[here.z]
 
     def pack_group(step):
         g = lax.rem(group + step, N_GROUP)
@@ -297,11 +301,16 @@
     keep.start()
     go_group(out_buf, in_buf, route_send, route_recv, 0, 1)
     lax.fori_loop(1, 4, route_step, 0)
-    drain(z_ids.at[:, pl.ds(0, GZ - 1)], id_recv.at[0])
+    drain(z_ids.at[pl.ds(0, GZ - 1)], id_recv.at[0])
+    for pair in range(8):
+        for k in range(4):
+            first, second = halves(z_ids[2 * k, pair], z_ids[2 * k + 1, pair])
+            plane_ids[2 * pair, k] = first
+            plane_ids[2 * pair + 1, k] = second
     for shift in PLANE:
         other = here.plane_at(shift)
-        send(z_ids.at[other], all_ids.at[here.plane], id_send.at[1], id_recv.at[1], here.at(shift))
-    all_ids[here.plane] = z_ids[here.plane]
+        send(plane_ids.at[other], all_ids.at[here.plane], id_send.at[1], id_recv.at[1], here.at(shift))
+    all_ids[here.plane] = plane_ids[here.plane]
     lax.fori_loop(4, N_GROUP, route_step, 0)
 
     z = iota((256, 256), 0)
@@ -312,8 +321,6 @@
     count = jnp.sum(jnp.sum(mask, axis=0, keepdims=True), axis=1, keepdims=True)
 
     total[...] = jnp.zeros_like(total)
-    low = iota((1, 128), 1) < 64
-    first_core = lax.rem(here.z, 2) == 0
     drain(all_ids.at[pl.ds(0, N_XY - 1)], id_recv.at[1])
 
     def collect(step, carry):
@@ -324,10 +331,7 @@
             top, bottom = halves(in_buf[g * GROUP + t], in_buf[g * GROUP + t + 1])
             tops.append(top)
             bottoms.append(bottom)
-            one, two = (all_ids[g * 2 + k // GZ, k % GZ] for k in (t, t + 1))
-            in_first = jnp.where(low, one, pltpu.roll(two, 64, 1))
-            in_second = jnp.where(low, pltpu.roll(one, 64, 1), two)
-            rows.append(jnp.where(first_core, in_first, in_second))
+            rows.append(all_ids[g * 2 + t // GZ, (t % GZ) // 2])
         tags = jnp.concatenate(rows, axis=1)
         tag_buf[g] = tags
         x = jnp.concatenate(
@@ -483,6 +487,13 @@
         send(w_out.at[to], w_in.at[here.z], w_send.at[0], w_recv.at[0], here.at(shift))
     w_in[here.z] = w_out[here.z]
     halo_finish(here, g_cells, g_ends_in, g_recv, g_edges, g_stack)
+    drain(w_in.at[pl.ds(0, GZ - 1)], w_recv.at[0])
+    for t in range(TILES):
+        p_out[t] = add_tiles([w_in[k, t] for k in range(GZ)])
+    for shift in PLANE:
+        to = here.plane_at(shift)
+        send(p_out.at[to], p_in.at[here.plane], w_send.at[1], w_recv.at[1], here.at(shift))
+    p_in[here.plane] = p_out[here.plane]
 
     def back(h, carry):
         slab = jnp.concatenate(
@@ -498,13 +509,11 @@
         return carry
 
     lax.fori_loop(0, 2, back, 0)
-    drain(w_in.at[pl.ds(0, GZ - 1)], w_recv.at[0])
-    for t in range(TILES):
-        p_out[t] = add_tiles([w_in[k, t] for k in range(GZ)])
+    drain(p_in.at[pl.ds(0, N_XY - 1)], w_recv.at[1])
+    f_buf[here.plane] = (add_tiles([p_in[k] for k in range(N_XY)]) * scale).astype(BF16)
     for shift in PLANE:
-        to = here.plane_at(shift)
-        send(p_out.at[to], p_in.at[here.plane], w_send.at[1], w_recv.at[1], here.at(shift))
-    p_in[here.plane] = p_out[here.plane]
+        at = f_buf.at[here.plane]
+        send(at, at, w_send.at[2], w_recv.at[2], here.at(shift))
 
     def spread_out(step):
         g = lax.rem(group + step, N_GROUP)
@@ -530,19 +539,13 @@
     keep_home.start()
     go_group(home_out, home_in, home_send, home_recv, 0, 1)
     spread_out(1)
-    drain(p_in.at[pl.ds(0, N_XY - 1)], w_recv.at[1])
-    f_buf[here.plane] = add_tiles([p_in[k] for k in range(N_XY)]) * scale
-    for shift in PLANE:
-        at = f_buf.at[here.plane]
-        send(at, at, w_send.at[2], w_recv.at[2], here.at(shift))
-    lax.fori_loop(2, 4, spread_step, 0)
+    lax.fori_loop(2, 3, spread_step, 0)
     drain(f_buf.at[pl.ds(0, N_XY - 1)], w_recv.at[2])
     for shift in COLUMN:
         whole = f_buf.at[pl.ds(0, TILES)]
         send(whole, a_buf.at[here.z], w_send.at[3], w_recv.at[3], here.at(shift))
-    for t in range(TILES):
-        a_buf[here.z, t] = f_buf[t]
-    lax.fori_loop(4, N_GROUP, spread_step, 0)
+    a_buf[here.z] = f_buf[0:TILES]
+    lax.fori_loop(3, N_GROUP, spread_step, 0)
     go_group(home_out, home_in, home_send, home_recv, N_GROUP - 1, 0)
 
     for g in range(N_GROUP):
@@ -550,7 +553,7 @@
     drain(a_buf.at[pl.ds(0, GZ - 1)], w_recv.at[3])
     most = pl.ds(0, N_DEV - 1)
     drain(out_buf.at[most], route_send.at[0])
-    drain(z_ids.at[:, pl.ds(0, GZ - 1)], id_send.at[0])
+    drain(z_ids.at[pl.ds(0, GZ - 1)], id_send.at[0])
     drain(all_ids.at[pl.ds(0, N_XY - 1)], id_send.at[1])
     halo_drain(cells, ends_in, halo_send)
     halo_drain(g_cells, g_ends_in, g_send)
@@ -570,7 +573,7 @@
         block_kernel,
         out_shape=(
             shaped((N_DEV, 16, 128), BF16),
-            shaped((GZ, TILES, 8, 128), F32),
+            shaped((GZ, TILES, 8, 128), BF16),
             shaped((64, 512), BF16),
             shaped((1, 128), F32),
         ),
@@ -579,9 +582,10 @@
         scratch_shapes=[
             pltpu.VMEM((N_DEV, 16, 128), BF16),
             pltpu.VMEM((N_DEV, 16, 128), BF16),
-            pltpu.VMEM((4, N_XY, 1, 128), jnp.int32),
-            pltpu.VMEM((N_XY, GZ, 1, 128), jnp.int32),
-            pltpu.VMEM((N_XY, GZ, 1, 128), jnp.int32),
+            pltpu.VMEM((GZ, N_XY // 2, 1, 128), jnp.int32),
+            pltpu.VMEM((GZ, N_XY // 2, 1, 128), jnp.int32),
+            pltpu.VMEM((N_XY, GZ // 2, 1, 128), jnp.int32),
+            pltpu.VMEM((N_XY, GZ // 2, 1, 128), jnp.int32),
             pltpu.VMEM((N_GROUP, 1, CHUNK), jnp.int32),
             pltpu.VMEM((N_GROUP, 256, CHUNK), BF16),
             pltpu.VMEM((512, 256), F32),
@@ -613,7 +617,7 @@
             pltpu.VMEM((GZ, TILES, 8, 128), F32),
             pltpu.VMEM((N_XY, 8, 128), F32),
             pltpu.VMEM((N_XY, 8, 128), F32),
-            pltpu.VMEM((N_XY, 8, 128), F32),
+            pltpu.VMEM((N_XY, 8, 128), BF16),
             pltpu.VMEM((N_DEV, 16, 128), BF16),
             dma((1,)), dma((N_GROUP,)), dma((2,)), dma((2,)), dma((2,)), dma((2,)), dma((2,)), dma((2,)),
             dma((2,)), dma((2,)), dma((2,)), dma((2,)), dma((4,)), dma((4,)), dma((1,)), dma((N_GROUP,)),
@@ -635,10 +639,10 @@
     for k in range(GZ):
         rows = slice(8 * k, 8 * k + 8)
         for t in range(6):
-            sub_ref[rows, 128 * t : 128 * t + 128] = sums_ref[k, t]
-        sub_ref[rows, 768:864] = sums_ref[k, 6][:, :96]
+            sub_ref[rows, 128 * t : 128 * t + 128] = sums_ref[k, t].astype(F32)
+        sub_ref[rows, 768:864] = sums_ref[k, 6].astype(F32)[:, :96]
         for t in range(4):
-            down_ref[rows, 128 * t : 128 * t + 128] = sums_ref[k, 7 + t]
+            down_ref[rows, 128 * t : 128 * t + 128] = sums_ref[k, 7 + t].astype(F32)
     coarse = coarse_ref[...].astype(F32)
     parts = [coarse[:, 128 * u : 128 * u + 128].reshape(64, 1, 128) for u in range(4)]
     fine_ref[...] = jnp.concatenate(parts, axis=1).reshape(64, 2, 2, 128).astype(BF16)

time: 89.1 us -> 86.7 us (0.973)
  Pallas kernels: 88.4 us -> 85.9 us
    pallas_call x1, Pallas kernels: 85.5 us -> 83.1 us  [block(): pl.pallas_call(block_kernel, out_shape=(shaped((N_DEV, 16, 128), BF16), s...]
where the time goes in v5:
time: 86.7 us; the launch traced here: 86.5 us
  Pallas kernels  85.9 us (99%)
    pallas_call x1, Pallas kernels, block(): pl.pallas_call(block_kernel, out_shape=(shaped((N_DEV, 16, 128), BF16), s...  83.1 us
    pallas_call x1, Pallas kernels, on_device(): pl.pallas_call(finish_kernel, out_shape=(shaped((32, 8192), BF16), shaped...  2.79 us

profile of v5, /device:TPU:1, one launch (start us, length us, event | category | flops | bytes accessed | tf_op | source)
XLA Modules:
  0.0 86.5 jit_solution(16962760765169451869)
XLA Ops:
  0.6 83.1 %block.1 = (bf16[128,16,128]{2,1,0:T(8,128)(2,1)}, bf16[8,11,8,128]{3,2,1,0:T(8,128)(2,1)}, bf16[64,512]{1,0:T(8,128)(2,1)}, f32[1,128]{1,0:T(1,128)}) custom-call(bf16[32,8192]{1,0:T(8,128)(2,1)} %feats_ref.1, s32[64,128]{1,0:T(8,128)} %bitcast.5, s32[1,128]{1,0:T(1,128)} %counts_ref.1, s32[4,4,256]{2,1,0:T(4,128)} %active_ref.1, ...), custom_call_target="tpu_custom_call" | custom-call | tf_op jit(solution)/shard_map/block/pallas_call | solution.py:572
  83.8 2.8 %finish.1 = (bf16[32,8192]{1,0:T(8,128)(2,1)}, bf16[64,2,2,128]{3,2,1,0:T(2,128)(2,1)}, f32[64,864]{1,0:T(8,128)}, f32[64,512]{1,0:T(8,128)}, f32[1,64]{1,0:T(1,128)}, /*index=5*/f32[1,64]{1,0:T(1,128)}) custom-call(bf16[128,16,128]{2,1,0:T(8,128)(2,1)} %get-tuple-element.16.home_ref, bf16[8,11,8,128]{3,2,1,0:T(8,128)(2,1)} %get-tuple-element.17.sums_ref, ...), custom_call_target="tpu_custom_call" | custom-call | tf_op jit(solution)/shard_map/finish/pallas_call | solution.py:668

commit v6 on v5

--- a/solution.py
+++ b/solution.py
@@ -12,6 +12,7 @@
 BF16 = jnp.bfloat16
 LOGICAL = pl.DeviceIdType.LOGICAL
 VMEM = pl.BlockSpec(memory_space=pltpu.VMEM)
+HBM = pl.BlockSpec(memory_space=pl.ANY)
 NT = (((1,), (1,)), ((), ()))
 TN = (((0,), (0,)), ((), ()))
 GX, GY, GZ = 4, 4, 8
@@ -79,10 +80,6 @@
 
 def halo_start(here, cells, ends, ends_in, send_sem, recv_sem):
     chan = cells.shape[2]
-    for shift in SIDES:
-        a, b, _ = shift
-        src, dst = cells.at[FROM[a], FROM[b]], cells.at[INTO[a], INTO[b]]
-        send(src, dst, send_sem.at[0], recv_sem.at[0], here.at(shift))
     for k, half, edge in ((0, 0, 0), (1, 128, 127)):
         faces = jnp.concatenate(
             [cells[1 + v // 4, 1 + v % 4, :, half : half + 128] for v in range(16)], axis=0
@@ -95,6 +92,10 @@
                 slot = (1 - a) * 3 + (1 - b)
                 to = here.at((a, b, c))
                 send(ends.at[k], ends_in.at[k, slot], send_sem.at[1], recv_sem.at[1], to)
+    for shift in SIDES:
+        a, b, _ = shift
+        src, dst = cells.at[FROM[a], FROM[b]], cells.at[INTO[a], INTO[b]]
+        send(src, dst, send_sem.at[0], recv_sem.at[0], here.at(shift))
 
 
 def halo_drain(cells, ends_in, sems):
@@ -102,18 +103,25 @@
     drain(ends_in, sems.at[1])
 
 
-def halo_finish(here, cells, ends_in, recv_sem, edges, stack):
-    halo_drain(cells, ends_in, recv_sem)
+def stack_cell(cells, edges, stack, x, y):
     chan = cells.shape[2]
-    for index, last, along_x in ((here.x, GX - 1, True), (here.y, GY - 1, False)):
-        for edge, outside in ((0, 0), (last, 5)):
-
-            @pl.when(index == edge)
-            def _():
-                for k in range(6):
-                    spot = (outside, k) if along_x else (k, outside)
-                    cells[spot] = jnp.zeros((chan, 256), BF16)
-
+    v = 6 * x + y
+    lane = iota((chan, 128), 1)
+    even = cells[x, y, :, 0:128]
+    odd = cells[x, y, :, 128:256]
+    prev = jnp.where(lane == 0, edges[1, v], pltpu.roll(odd.astype(F32), 1, 1))
+    nxt = jnp.where(lane == 127, edges[0, v], pltpu.roll(even.astype(F32), 127, 1))
+    stack[v, 0:chan, 0:128] = prev.astype(BF16)
+    stack[v, 0:chan, 128:256] = even
+    stack[v, chan : 2 * chan, 0:128] = even
+    stack[v, chan : 2 * chan, 128:256] = odd
+    stack[v, 2 * chan : 3 * chan, 0:128] = odd
+    stack[v, 2 * chan : 3 * chan, 128:256] = nxt.astype(BF16)
+
+
+def halo_inner(here, cells, ends_in, recv_sem, edges, stack):
+    drain(ends_in, recv_sem.at[1])
+    chan = cells.shape[2]
     inside_x = {-1: (here.x > 0).astype(F32), 0: 1.0, 1: (here.x < GX - 1).astype(F32)}
     inside_y = {-1: (here.y > 0).astype(F32), 0: 1.0, 1: (here.y < GY - 1).astype(F32)}
     inside_z = ((here.z < GZ - 1).astype(F32), (here.z > 0).astype(F32))
@@ -135,23 +143,38 @@
         for x in range(6):
             for y in range(6):
                 edges[k, x * 6 + y] = spread[y * chan : (y + 1) * chan, 128 * x : 128 * x + 128]
-    lane = iota((chan, 128), 1)
 
     def body(v, carry):
-        x, y = lax.div(v, 6), lax.rem(v, 6)
-        even = cells[x, y, :, 0:128]
-        odd = cells[x, y, :, 128:256]
-        prev = jnp.where(lane == 0, edges[1, v], pltpu.roll(odd.astype(F32), 1, 1))
-        nxt = jnp.where(lane == 127, edges[0, v], pltpu.roll(even.astype(F32), 127, 1))
-        stack[v, 0:chan, 0:128] = prev.astype(BF16)
-        stack[v, 0:chan, 128:256] = even
-        stack[v, chan : 2 * chan, 0:128] = even
-        stack[v, chan : 2 * chan, 128:256] = odd
-        stack[v, 2 * chan : 3 * chan, 0:128] = odd
-        stack[v, 2 * chan : 3 * chan, 128:256] = nxt.astype(BF16)
-        return carry
-
-    lax.fori_loop(0, 36, body, 0, unroll=4)
+        stack_cell(cells, edges, stack, 1 + lax.div(v, 4), 1 + lax.rem(v, 4))
+        return carry
+
+    lax.fori_loop(0, 16, body, 0, unroll=4)
+
+
+def halo_outer(here, cells, recv_sem, edges, stack):
+    drain(cells.at[pl.ds(0, 5), pl.ds(0, 4)], recv_sem.at[0])
+    chan = cells.shape[2]
+    for index, last, along_x in ((here.x, GX - 1, True), (here.y, GY - 1, False)):
+        for edge, outside in ((0, 0), (last, 5)):
+
+            @pl.when(index == edge)
+            def _():
+                for k in range(6):
+                    spot = (outside, k) if along_x else (k, outside)
+                    cells[spot] = jnp.zeros((chan, 256), BF16)
+
+    def body(k, carry):
+        stack_cell(cells, edges, stack, 0, k)
+        stack_cell(cells, edges, stack, 5, k)
+        return carry
+
+    def side(k, carry):
+        stack_cell(cells, edges, stack, 1 + k, 0)
+        stack_cell(cells, edges, stack, 1 + k, 5)
+        return carry
+
+    lax.fori_loop(0, 6, body, 0, unroll=2)
+    lax.fori_loop(0, 4, side, 0, unroll=2)
 
 
 def patches(stack, v):
@@ -228,14 +251,14 @@
 
 
 def block_kernel(
-    feats_ref, ids_ref, counts_ref, active_ref, w_sub_ref, w_down_ref, gain_ref, shift_ref, ct_ref,
+    feats_at, ids_ref, counts_ref, active_ref, w_sub_at, w_down_at, gain_ref, shift_ref, ct_at,
     home_in, a_buf, coarse_ref, vector_out,
-    out_buf, in_buf, out_ids, z_ids, plane_ids, all_ids, tag_buf, pick_buf, total, back_grid, mask_ref, w_band, w_back, w_down_t,
+    feats_ref, w_sub_ref, w_down_ref, ct_ref, out_buf, in_buf, out_ids, z_ids, plane_ids, all_ids, tag_buf, pick_buf, total, back_grid, mask_ref, w_band, w_back, w_down_t,
     cells, ends, ends_in, edges, stack, hid, fine, g_fine, gc_all,
     g_cells, g_ends, g_ends_in, g_edges, g_stack,
     z_one, xy_one, z_two, xy_two, sub_acc,
     w_out, w_in, p_out, p_in, f_buf, home_out,
-    route_send, route_recv, id_send, id_recv, halo_send, halo_recv, g_send, g_recv,
+    load_sem, route_send, route_recv, id_send, id_recv, halo_send, halo_recv, g_send, g_recv,
     one_send, one_recv, two_send, two_recv, w_send, w_recv, home_send, home_recv,
 ):
     here = Place()
@@ -243,6 +266,10 @@
     group = lax.div(me, GROUP)
     member = lax.rem(me, GROUP)
     barrier = pltpu.get_barrier_semaphore()
+    pairs = ((feats_at, feats_ref), (w_sub_at, w_sub_ref), (w_down_at, w_down_ref), (ct_at, ct_ref))
+    loads = [pltpu.make_async_copy(a, b, load_sem.at[k]) for k, (a, b) in enumerate(pairs)]
+    for load in loads:
+        load.start()
 
     def greet(step, carry):
         pl.semaphore_signal(
@@ -281,6 +308,8 @@
         k = here.zs[shift[2]]
         send(out_ids.at[k], z_ids.at[here.z], id_send.at[0], id_recv.at[0], here.at(shift))
     z_ids[here.z] = out_ids[here.z]
+
+    loads[0].wait()
 
     def pack_group(step):
         g = lax.rem(group + step, N_GROUP)
@@ -351,6 +380,8 @@
         cells[1 + v // 4, 1 + v % 4] = (total[32 * v : 32 * v + 32, :] * mask[v : v + 1]).astype(BF16)
     halo_start(here, cells, ends, ends_in, halo_send, halo_recv)
 
+    for load in loads[1:]:
+        load.wait()
     weights = w_sub_ref[...].astype(F32)
     for p in range(4):
         parts = [jnp.zeros((64, 288 * k), F32) for k in (p, 3 - p)]
@@ -391,29 +422,38 @@
                     v = (2 * up + a) * 4 + 2 * uq + b
                     g_fine[v, :, 128 * c : 128 * c + 128] = pulled[at : at + 64]
 
-    halo_finish(here, cells, ends_in, halo_recv, edges, stack)
+    halo_inner(here, cells, ends_in, halo_recv, edges, stack)
+    halo_outer(here, cells, halo_recv, edges, stack)
     one_bufs = (z_one, xy_one, one_send, one_recv)
     two_bufs = (z_two, xy_two, two_send, two_recv)
 
-    def conv(q, acc):
+    def conv(q):
         slab = jnp.concatenate([stack[pl.ds(6 * x + q, 3)].reshape(288, 256) for x in range(6)], axis=0)
         out = jnp.dot(w_band[...], slab, preferred_element_type=F32)
+        masks = [mask_ref[pl.ds(4 * p + q, 1), :] for p in range(4)]
+        parts = [out[64 * p : 64 * p + 64] * masks[p] for p in range(4)]
         for p in range(4):
-            v = 4 * p + q
-            part = out[64 * p : 64 * p + 64] * mask_ref[pl.ds(v, 1), :]
-            hid[v] = part
-            acc = acc + fold(part)
-        return acc
-
-    summed = lax.fori_loop(0, 4, conv, jnp.zeros((64, 128), F32))
-    own_mean = jnp.sum(summed, axis=1, keepdims=True) / jnp.maximum(count, 1.0)
-
-    def spread(v, acc):
-        gap = (hid[v] - own_mean) * mask_ref[pl.ds(v, 1), :]
-        return acc + fold(gap * gap)
-
-    square = lax.fori_loop(0, 16, spread, jnp.zeros((64, 128), F32))
-    combine_start(here, moments(to_row(summed), to_row(square), count), one_bufs)
+            hid[4 * p + q] = parts[p]
+        return parts, masks
+
+    def gather_sums(parts, masks, sums):
+        acc, square = sums
+        for part, on in zip(parts, masks):
+            gap = (part - about) * on
+            acc = acc + fold(gap)
+            square = square + fold(gap * gap)
+        return acc, square
+
+    parts, masks = conv(0)
+    near_count = jnp.sum(add_tiles(list(masks)), axis=1, keepdims=True)
+    about = jnp.sum(fold(add_tiles(list(parts))), axis=1, keepdims=True) / jnp.maximum(near_count, 1.0)
+    zero = jnp.zeros((64, 128), F32)
+    sums = gather_sums(parts, masks, (zero, zero))
+    gaps, square = lax.fori_loop(1, 4, lambda q, sums: gather_sums(*conv(q), sums), sums)
+    about_row, gap_row = to_row(jnp.where(iota((64, 128), 1) == 0, about, 0.0)), to_row(gaps)
+    summed_row = gap_row + count * about_row
+    square_row = jnp.maximum(to_row(square) - gap_row * gap_row / jnp.maximum(count, 1.0), 0.0)
+    combine_start(here, moments(summed_row, square_row, count), one_bufs)
     gain, shift = to_col(gain_ref[...]), to_col(shift_ref[...])
     merged = combine_finish(here, merge_moments, one_bufs)
     n_active = jnp.where(iota((1, 128), 1) < 64, counts_of(merged), merged[0:1])
@@ -438,7 +478,6 @@
         g_fine[v] = grad
         return sums[0] + fold(grad), sums[1] + fold(grad * normed)
 
-    zero = jnp.zeros((64, 128), F32)
     sum_shift, sum_gain = lax.fori_loop(0, 16, norm, (zero, zero))
     combine_start(here, to_row(sum_shift, sum_gain), two_bufs)
     down = jnp.zeros((64, 512), F32)
@@ -486,7 +525,8 @@
         to = here.zs[shift[2]]
         send(w_out.at[to], w_in.at[here.z], w_send.at[0], w_recv.at[0], here.at(shift))
     w_in[here.z] = w_out[here.z]
-    halo_finish(here, g_cells, g_ends_in, g_recv, g_edges, g_stack)
+    halo_inner(here, g_cells, g_ends_in, g_recv, g_edges, g_stack)
+    halo_outer(here, g_cells, g_recv, g_edges, g_stack)
     drain(w_in.at[pl.ds(0, GZ - 1)], w_recv.at[0])
     for t in range(TILES):
         p_out[t] = add_tiles([w_in[k, t] for k in range(GZ)])
@@ -577,9 +617,13 @@
             shaped((64, 512), BF16),
             shaped((1, 128), F32),
         ),
-        in_specs=[VMEM] * 9,
+        in_specs=[HBM, VMEM, VMEM, VMEM, HBM, HBM, VMEM, VMEM, HBM],
         out_specs=(VMEM,) * 4,
         scratch_shapes=[
+            pltpu.VMEM((32, 8192), BF16),
+            pltpu.VMEM((64, 864), BF16),
+            pltpu.VMEM((64, 512), BF16),
+            pltpu.VMEM((64, 2, 2, 128), BF16),
             pltpu.VMEM((N_DEV, 16, 128), BF16),
             pltpu.VMEM((N_DEV, 16, 128), BF16),
             pltpu.VMEM((GZ, N_XY // 2, 1, 128), jnp.int32),
@@ -619,7 +663,7 @@
             pltpu.VMEM((N_XY, 8, 128), F32),
             pltpu.VMEM((N_XY, 8, 128), BF16),
             pltpu.VMEM((N_DEV, 16, 128), BF16),
-            dma((1,)), dma((N_GROUP,)), dma((2,)), dma((2,)), dma((2,)), dma((2,)), dma((2,)), dma((2,)),
+            dma((4,)), dma((1,)), dma((N_GROUP,)), dma((2,)), dma((2,)), dma((2,)), dma((2,)), dma((2,)), dma((2,)),
             dma((2,)), dma((2,)), dma((2,)), dma((2,)), dma((4,)), dma((4,)), dma((1,)), dma((N_GROUP,)),
         ],
         compiler_params=pltpu.CompilerParams(collective_id=0, has_side_effects=True),
@@ -636,6 +680,7 @@
         return carry
 
     lax.fori_loop(0, 64, unpack, 0, unroll=8)
+
     for k in range(GZ):
         rows = slice(8 * k, 8 * k + 8)
         for t in range(6):

time: 86.7 us -> 85.1 us (0.982)
  Pallas kernels: 85.9 us -> 84.3 us
    pallas_call x1, Pallas kernels: 83.1 us -> 81.5 us  [block(): pl.pallas_call(block_kernel, out_shape=(shaped((N_DEV, 16, 128), BF16), s...]
where the time goes in v6:
time: 85.1 us; the launch traced here: 84.9 us
  Pallas kernels  84.3 us (99%)
    pallas_call x1, Pallas kernels, block(): pl.pallas_call(block_kernel, out_shape=(shaped((N_DEV, 16, 128), BF16), s...  81.5 us
    pallas_call x1, Pallas kernels, on_device(): pl.pallas_call(finish_kernel, out_shape=(shaped((32, 8192), BF16), shaped...  2.79 us

profile of v6, /device:TPU:1, one launch (start us, length us, event | category | flops | bytes accessed | tf_op | source)
XLA Modules:
  0.0 84.9 jit_solution(250707685924036578)
XLA Ops:
  0.6 81.5 %block.1 = (bf16[128,16,128]{2,1,0:T(8,128)(2,1)}, bf16[8,11,8,128]{3,2,1,0:T(8,128)(2,1)}, bf16[64,512]{1,0:T(8,128)(2,1)}, f32[1,128]{1,0:T(1,128)}) custom-call(bf16[32,8192]{1,0:T(8,128)(2,1)} %feats_at.1, s32[64,128]{1,0:T(8,128)} %bitcast.5, s32[1,128]{1,0:T(1,128)} %counts_ref.1, s32[4,4,256]{2,1,0:T(4,128)} %active_ref.1, bf16[64,864]{1,0:T(8,128)(2,1)} %w_sub_at.1, ...), custom_call_target="tpu_custom_call" | custom-call | tf_op jit(solution)/shard_map/block/pallas_call | solution.py:612
  82.1 2.8 %finish.1 = (bf16[32,8192]{1,0:T(8,128)(2,1)}, bf16[64,2,2,128]{3,2,1,0:T(2,128)(2,1)}, f32[64,864]{1,0:T(8,128)}, f32[64,512]{1,0:T(8,128)}, f32[1,64]{1,0:T(1,128)}, /*index=5*/f32[1,64]{1,0:T(1,128)}) custom-call(bf16[128,16,128]{2,1,0:T(8,128)(2,1)} %get-tuple-element.16.home_ref, bf16[8,11,8,128]{3,2,1,0:T(8,128)(2,1)} %get-tuple-element.17.sums_ref, ...), custom_call_target="tpu_custom_call" | custom-call | tf_op jit(solution)/shard_map/finish/pallas_call | solution.py:713

commit v7 on v6

--- a/solution.py
+++ b/solution.py
@@ -12,7 +12,7 @@
 BF16 = jnp.bfloat16
 LOGICAL = pl.DeviceIdType.LOGICAL
 VMEM = pl.BlockSpec(memory_space=pltpu.VMEM)
-HBM = pl.BlockSpec(memory_space=pl.ANY)
+HBM = pl.BlockSpec(memory_space=pltpu.HBM)
 NT = (((1,), (1,)), ((), ()))
 TN = (((0,), (0,)), ((), ()))
 GX, GY, GZ = 4, 4, 8
@@ -251,9 +251,9 @@
 
 
 def block_kernel(
-    feats_at, ids_ref, counts_ref, active_ref, w_sub_at, w_down_at, gain_ref, shift_ref, ct_at,
+    feats_at, ids_at, counts_at, active_at, w_sub_at, w_down_at, gain_at, shift_at, ct_at,
     home_in, a_buf, coarse_ref, vector_out,
-    feats_ref, w_sub_ref, w_down_ref, ct_ref, out_buf, in_buf, out_ids, z_ids, plane_ids, all_ids, tag_buf, pick_buf, total, back_grid, mask_ref, w_band, w_back, w_down_t,
+    ids_ref, counts_ref, feats_ref, active_ref, gain_ref, shift_ref, w_sub_ref, w_down_ref, ct_ref, out_buf, in_buf, out_ids, z_ids, plane_ids, all_ids, tag_buf, pick_buf, total, back_grid, mask_ref, w_band, w_back, w_down_t,
     cells, ends, ends_in, edges, stack, hid, fine, g_fine, gc_all,
     g_cells, g_ends, g_ends_in, g_edges, g_stack,
     z_one, xy_one, z_two, xy_two, sub_acc,
@@ -266,7 +266,10 @@
     group = lax.div(me, GROUP)
     member = lax.rem(me, GROUP)
     barrier = pltpu.get_barrier_semaphore()
-    pairs = ((feats_at, feats_ref), (w_sub_at, w_sub_ref), (w_down_at, w_down_ref), (ct_at, ct_ref))
+    pairs = (
+        (ids_at, ids_ref), (counts_at, counts_ref), (feats_at, feats_ref), (active_at, active_ref),
+        (gain_at, gain_ref), (shift_at, shift_ref), (w_sub_at, w_sub_ref), (w_down_at, w_down_ref), (ct_at, ct_ref),
+    )
     loads = [pltpu.make_async_copy(a, b, load_sem.at[k]) for k, (a, b) in enumerate(pairs)]
     for load in loads:
         load.start()
@@ -280,6 +283,8 @@
     lax.fori_loop(1, N_DEV, greet, 0, unroll=True)
 
     row, lane = iota((64, 128), 0), iota((64, 128), 1)
+    loads[0].wait()
+    loads[1].wait()
     counts = counts_ref[...]
     even = jnp.sum(jnp.where(lane == 2 * row, counts, 0), axis=1, keepdims=True)
     odd = jnp.sum(jnp.where(lane == 2 * row + 1, counts, 0), axis=1, keepdims=True)
@@ -309,7 +314,7 @@
         send(out_ids.at[k], z_ids.at[here.z], id_send.at[0], id_recv.at[0], here.at(shift))
     z_ids[here.z] = out_ids[here.z]
 
-    loads[0].wait()
+    loads[2].wait()
 
     def pack_group(step):
         g = lax.rem(group + step, N_GROUP)
@@ -344,6 +349,7 @@
 
     z = iota((256, 256), 0)
     order = jnp.where((z >> 1) + (z & 1) * 128 == iota((256, 256), 1), 1.0, 0.0)
+    loads[3].wait()
     active = jnp.concatenate([active_ref[p] for p in range(4)], axis=0).astype(F32)
     mask = jnp.dot(active.astype(BF16), order.astype(BF16), preferred_element_type=F32)
     mask_ref[...] = mask
@@ -380,7 +386,7 @@
         cells[1 + v // 4, 1 + v % 4] = (total[32 * v : 32 * v + 32, :] * mask[v : v + 1]).astype(BF16)
     halo_start(here, cells, ends, ends_in, halo_send, halo_recv)
 
-    for load in loads[1:]:
+    for load in loads[4:]:
         load.wait()
     weights = w_sub_ref[...].astype(F32)
     for p in range(4):
@@ -617,10 +623,15 @@
             shaped((64, 512), BF16),
             shaped((1, 128), F32),
         ),
-        in_specs=[HBM, VMEM, VMEM, VMEM, HBM, HBM, VMEM, VMEM, HBM],
+        in_specs=[HBM] * 9,
         out_specs=(VMEM,) * 4,
         scratch_shapes=[
+            pltpu.VMEM((64, 128), jnp.int32),
+            pltpu.VMEM((1, 128), jnp.int32),
             pltpu.VMEM((32, 8192), BF16),
+            pltpu.VMEM((4, 4, 256), jnp.int32),
+            pltpu.VMEM((1, 64), F32),
+            pltpu.VMEM((1, 64), F32),
             pltpu.VMEM((64, 864), BF16),
             pltpu.VMEM((64, 512), BF16),
             pltpu.VMEM((64, 2, 2, 128), BF16),
@@ -663,12 +674,14 @@
             pltpu.VMEM((N_XY, 8, 128), F32),
             pltpu.VMEM((N_XY, 8, 128), BF16),
             pltpu.VMEM((N_DEV, 16, 128), BF16),
-            dma((4,)), dma((1,)), dma((N_GROUP,)), dma((2,)), dma((2,)), dma((2,)), dma((2,)), dma((2,)), dma((2,)),
+            dma((9,)), dma((1,)), dma((N_GROUP,)), dma((2,)), dma((2,)), dma((2,)), dma((2,)), dma((2,)), dma((2,)),
             dma((2,)), dma((2,)), dma((2,)), dma((2,)), dma((4,)), dma((4,)), dma((1,)), dma((N_GROUP,)),
         ],
-        compiler_params=pltpu.CompilerParams(collective_id=0, has_side_effects=True),
+        compiler_params=pltpu.CompilerParams(
+            collective_id=0, has_side_effects=True, vmem_limit_bytes=36 << 20
+        ),
         name="block",
-    )(*operands)
+    )(*(pltpu.with_memory_space_constraint(x, pltpu.HBM) for x in operands))
 
 
 def finish_kernel(home_ref, sums_ref, coarse_ref, vector_ref, points_ref, fine_ref, sub_ref, down_ref, gain_ref, shift_ref):
@@ -722,6 +735,7 @@
         ),
         in_specs=[VMEM] * 4,
         out_specs=(VMEM,) * 6,
+        compiler_params=pltpu.CompilerParams(vmem_limit_bytes=8 << 20),
         name="finish",
     )(*parts)
     return coarse, points, grad_sub, grad_down, grad_gain.reshape(64), grad_shift.reshape(64)

time: 85.1 us -> 82.5 us (0.969)
  Pallas kernels: 84.3 us -> 81.7 us
    pallas_call x1, Pallas kernels: 81.5 us -> 80.1 us  [block(): pl.pallas_call(block_kernel, out_shape=(shaped((N_DEV, 16, 128), BF16), s...]
    pallas_call x1, Pallas kernels: 2.79 us -> 1.65 us  [on_device(): pl.pallas_call(finish_kernel, out_shape=(shaped((32, 8192), BF16), shaped...]
where the time goes in v7:
time: 82.5 us; the launch traced here: 82.3 us
  Pallas kernels  81.7 us (99%)
    pallas_call x1, Pallas kernels, block(): pl.pallas_call(block_kernel, out_shape=(shaped((N_DEV, 16, 128), BF16), s...  80.1 us

profile of v7, /device:TPU:1, one launch (start us, length us, event | category | flops | bytes accessed | tf_op | source)
XLA Modules:
  0.0 82.3 jit_solution(5241363417884030354)
XLA Ops:
  0.6 80.1 %block.1 = (bf16[128,16,128]{2,1,0:T(8,128)(2,1)S(1)}, bf16[8,11,8,128]{3,2,1,0:T(8,128)(2,1)S(1)}, bf16[64,512]{1,0:T(8,128)(2,1)S(1)}, f32[1,128]{1,0:T(1,128)S(1)}) custom-call(bf16[32,8192]{1,0:T(8,128)(2,1)} %feats_at.1, s32[64,128]{1,0:T(8,128)} %bitcast.5, s32[1,128]{1,0:T(1,128)} %counts_at.1, s32[4,4,256]{2,1,0:T(4,128)} %active_at.1, ...), custom_call_target="tpu_custom_call" | custom-call | tf_op jit(solution)/shard_map/block/pallas_call | solution.py:618
  80.7 1.6 %finish.1 = (bf16[32,8192]{1,0:T(8,128)(2,1)}, bf16[64,2,2,128]{3,2,1,0:T(2,128)(2,1)}, f32[64,864]{1,0:T(8,128)}, f32[64,512]{1,0:T(8,128)}, f32[1,64]{1,0:T(1,128)}, /*index=5*/f32[1,64]{1,0:T(1,128)}) custom-call(bf16[128,16,128]{2,1,0:T(8,128)(2,1)S(1)} %get-tuple-element.16.home_ref, bf16[8,11,8,128]{3,2,1,0:T(8,128)(2,1)S(1)} %get-tuple-element.17.sums_ref, ...), custom_call_target="tpu_custom_call" | custom-call | tf_op jit(solution)/shard_map/finish/pallas_call | solution.py:726

commit v8 on v7

--- a/solution.py
+++ b/solution.py
@@ -555,12 +555,6 @@
         return carry
 
     lax.fori_loop(0, 2, back, 0)
-    drain(p_in.at[pl.ds(0, N_XY - 1)], w_recv.at[1])
-    f_buf[here.plane] = (add_tiles([p_in[k] for k in range(N_XY)]) * scale).astype(BF16)
-    for shift in PLANE:
-        at = f_buf.at[here.plane]
-        send(at, at, w_send.at[2], w_recv.at[2], here.at(shift))
-
     def spread_out(step):
         g = lax.rem(group + step, N_GROUP)
         column = tag_buf[g] >> 8
@@ -584,14 +578,19 @@
     keep_home = pltpu.make_async_copy(home_out.at[me], home_in.at[me], home_recv.at[group])
     keep_home.start()
     go_group(home_out, home_in, home_send, home_recv, 0, 1)
+    drain(p_in.at[pl.ds(0, N_XY - 1)], w_recv.at[1])
+    f_buf[here.plane] = (add_tiles([p_in[k] for k in range(N_XY)]) * scale).astype(BF16)
+    for shift in PLANE:
+        at = f_buf.at[here.plane]
+        send(at, at, w_send.at[2], w_recv.at[2], here.at(shift))
     spread_out(1)
-    lax.fori_loop(2, 3, spread_step, 0)
+    lax.fori_loop(2, 6, spread_step, 0)
     drain(f_buf.at[pl.ds(0, N_XY - 1)], w_recv.at[2])
     for shift in COLUMN:
         whole = f_buf.at[pl.ds(0, TILES)]
         send(whole, a_buf.at[here.z], w_send.at[3], w_recv.at[3], here.at(shift))
     a_buf[here.z] = f_buf[0:TILES]
-    lax.fori_loop(3, N_GROUP, spread_step, 0)
+    lax.fori_loop(6, N_GROUP, spread_step, 0)
     go_group(home_out, home_in, home_send, home_recv, N_GROUP - 1, 0)
 
     for g in range(N_GROUP):

time: 82.5 us -> 81.3 us (0.985)
  Pallas kernels: 81.7 us -> 80.6 us
    pallas_call x1, Pallas kernels: 80.1 us -> 78.9 us  [block(): pl.pallas_call(block_kernel, out_shape=(shaped((N_DEV, 16, 128), BF16), s...]
where the time goes in v8:
time: 81.3 us; the launch traced here: 81.2 us
  Pallas kernels  80.6 us (99%)
    pallas_call x1, Pallas kernels, block(): pl.pallas_call(block_kernel, out_shape=(shaped((N_DEV, 16, 128), BF16), s...  78.9 us
    pallas_call x1, Pallas kernels, on_device(): pl.pallas_call(finish_kernel, out_shape=(shaped((32, 8192), BF16), shaped...  1.65 us

profile of v8, /device:TPU:1, one launch (start us, length us, event | category | flops | bytes accessed | tf_op | source)
XLA Modules:
  0.0 81.2 jit_solution(7134282124791340515)
XLA Ops:
  0.6 78.9 %block.1 = (bf16[128,16,128]{2,1,0:T(8,128)(2,1)S(1)}, bf16[8,11,8,128]{3,2,1,0:T(8,128)(2,1)S(1)}, bf16[64,512]{1,0:T(8,128)(2,1)S(1)}, f32[1,128]{1,0:T(1,128)S(1)}) custom-call(bf16[32,8192]{1,0:T(8,128)(2,1)} %feats_at.1, s32[64,128]{1,0:T(8,128)} %bitcast.5, s32[1,128]{1,0:T(1,128)} %counts_at.1, s32[4,4,256]{2,1,0:T(4,128)} %active_at.1, ...), custom_call_target="tpu_custom_call" | custom-call | tf_op jit(solution)/shard_map/block/pallas_call | solution.py:617
  79.6 1.6 %finish.1 = (bf16[32,8192]{1,0:T(8,128)(2,1)}, bf16[64,2,2,128]{3,2,1,0:T(2,128)(2,1)}, f32[64,864]{1,0:T(8,128)}, f32[64,512]{1,0:T(8,128)}, f32[1,64]{1,0:T(1,128)}, /*index=5*/f32[1,64]{1,0:T(1,128)}) custom-call(bf16[128,16,128]{2,1,0:T(8,128)(2,1)S(1)} %get-tuple-element.16.home_ref, bf16[8,11,8,128]{3,2,1,0:T(8,128)(2,1)S(1)} %get-tuple-element.17.sums_ref, ...), custom_call_target="tpu_custom_call" | custom-call | tf_op jit(solution)/shard_map/finish/pallas_call | solution.py:725
